TPU v7x, 128 devices: a whole 4x4x4 slice. The times are simulated.
128 devices in a mesh: layer: 4 (over x), latent: 8 (over z, core), token: 4 (over y).
Axes of the slice: x: 4, y: 4, z: 4, core: 2. Of those that a mesh axis runs over, the one named last changes fastest.
Arguments:
- residuals: bfloat16 [4, 768, 2560], P('layer', 'token'), may hold values from -6 to 6
- enc_weight: bfloat16 [4, 2560, 8192], P('layer', None, 'latent'), may hold values from -0.125 to 0.125
- enc_bias: float32 [4, 8192], P('layer', 'latent'), may hold values from -1 to 0.5
- dec_weight: bfloat16 [4, 4, 8192, 2560], P('layer', None, 'latent', 'token'), may hold values from -0.0625 to 0.0625
- dec_bias: float32 [4, 2560], P('layer', 'token'), may hold values from -3 to 3
- targets: bfloat16 [4, 768, 2560], P('layer', 'latent', 'token'), may hold values from -6 to 6
Outputs:
- grad_dec: bfloat16 [4, 4, 8192, 2560], P('layer', None, 'latent', 'token')
- grad_enc: bfloat16 [4, 2560, 8192], P('layer', 'token', 'latent')
All inputs are finite; a program needn't handle non-finite values.
Results may differ from a plain program's by a relative error of at most 0.02.
Values may be sent and summed in bfloat16 or wider, within the bound.
No kernel may reach another device: no remote copies, remote signals or barrier semaphores. Data moves between devices by JAX's collectives and lax.ppermute only.
A program may use at most 128 MiB of HBM per device.

v0:
```python
import jax
import jax.numpy as jnp
from jax import lax
from jax.sharding import PartitionSpec as P


SQRT_HALF = 0.7071067811865476
DENSITY_NORM = 0.3989422804014327
LOSS_SCALE = 64.0
CHAINS = ((2, 3), (0, 1))
PARTS = ((0,), (1, 2, 3))
F32 = jnp.float32
BF16 = jnp.bfloat16


def gelu_value(values):
    return 0.5 * values * (1.0 + lax.erf(values * SQRT_HALF))


def gelu_slope(values):
    return (
        0.5 * (1.0 + lax.erf(values * SQRT_HALF))
        + values * jnp.exp(-0.5 * values * values) * DENSITY_NORM
    )


def swap_cores(value, n_latent):
    return lax.ppermute(value, "latent", [(i, i ^ 1) for i in range(n_latent)])


def exchange(value, axis, flips):
    n_latent = lax.axis_size("latent")
    pairs = []
    for i in range(n_latent):
        flip = flips[i % 2]
        if axis == "plane":
            pairs.append((i, ((i // 2) ^ flip) * 2 + i % 2))
        else:
            size = lax.axis_size(axis)
            if axis == "layer":
                pairs += [(j * n_latent + i, (j ^ flip) * n_latent + i) for j in range(size)]
            else:
                pairs += [(i * size + j, i * size + (j ^ flip)) for j in range(size)]
    names = {"plane": "latent", "layer": ("layer", "latent"), "token": ("latent", "token")}[axis]
    return lax.ppermute(value, names, pairs)


SIDE_A = (1, 3)
SIDE_B = (3, 1)


def body(residuals, enc_weight, enc_bias, dec_weight, dec_bias, targets):
    layers = lax.axis_size("layer")
    n_latent = lax.axis_size("latent")
    n_token = lax.axis_size("token")
    layer = lax.axis_index("layer")
    latent = lax.axis_index("latent")
    token = lax.axis_index("token")
    core = latent % 2
    plane = latent // 2
    planes = n_latent // 2
    side_a = 1 + 2 * core
    side_b = 3 - 2 * core
    res = residuals[0]
    rows = res.shape[0]
    tokens_all = rows * n_token
    weight = dec_weight[0]
    wid = weight.shape[2]
    half = rows // 2
    part = half // planes

    def by_core(mine, twin):
        return jnp.where(core == 0, mine, twin), jnp.where(core == 0, twin, mine)

    preact = jnp.dot(res, enc_weight[0], preferred_element_type=F32) + enc_bias[0]
    latents = gelu_value(preact).astype(BF16)
    near = exchange(latents, "token", SIDE_B)
    far = exchange(jnp.stack([latents, near]), "token", SIDE_A)
    one, three = by_core(far[0], near)
    lat = {0: latents, 1: one, 2: far[1], 3: three}
    own_term = dec_bias[0] - targets[0].astype(F32)
    own_shift = plane ^ token

    products = {}
    for ks in PARTS:
        lhs = jnp.concatenate([lat[k] for k in ks], axis=0) if len(ks) > 1 else lat[ks[0]]
        for m in range(layers):
            prod = jnp.dot(lhs, weight[m], preferred_element_type=F32).astype(BF16)
            prod = prod.reshape(len(ks), 2, half, wid)
            for at, k in enumerate(ks):
                products[m, k] = prod[at]

    ks = tuple(range(n_token))

    def chain(ms):
        nk, nm = len(ks), len(ms)
        targets_of = jnp.array(ms)
        live = (targets_of >= layer)[:, None, None, None]
        stacked = jnp.stack([jnp.stack([products[m, k] for k in ks]) for m in ms])
        keep = lax.dynamic_index_in_dim(stacked, core, 2, keepdims=False)
        send = lax.dynamic_index_in_dim(stacked, 1 - core, 2, keepdims=False)
        other = swap_cores(send, n_latent)
        total = keep.astype(F32) + other.astype(F32)
        mask = (targets_of == layer)[:, None] & (jnp.array(ks) == own_shift)[None, :]
        total = total + jnp.where(mask[:, :, None, None], own_term, 0.0)
        total = jnp.where(live, total, 0.0)
        total = total.astype(BF16).reshape(nm, nk, planes, part, wid)

        def piece(at):
            return lax.dynamic_index_in_dim(total, plane ^ at, 2, keepdims=False)

        got = exchange(jnp.stack([piece(side_a), piece(2)]), "plane", SIDE_A)
        pass_on = (piece(side_b).astype(F32) + got[1].astype(F32)).astype(BF16)
        summed = piece(0).astype(F32) + got[0].astype(F32)
        summed = summed + exchange(pass_on, "plane", SIDE_B).astype(F32)
        summed = summed.astype(BF16)
        first = 1 if ms[0] == 0 else 0
        upper = summed[first:]
        upper = (upper.astype(F32) + exchange(upper, "layer", SIDE_A).astype(F32)).astype(BF16)
        error = upper.astype(F32) + exchange(upper, "layer", SIDE_B).astype(F32)
        if first:
            error = jnp.concatenate([summed[:1].astype(F32), error])
        error = jnp.where(live, LOSS_SCALE / tokens_all * error, 0.0).astype(BF16)
        halves = jnp.zeros((nm, nk, planes, part, wid), BF16)
        near = exchange(error, "plane", SIDE_B)
        far = exchange(jnp.stack([error, near]), "plane", SIDE_A)
        pieces = [(error, 0), (near, side_b), (far[0], side_a), (far[1], 2)]
        for value, at in pieces:
            halves = lax.dynamic_update_index_in_dim(halves, value, plane ^ at, 2)
        halves = halves.reshape(nm, nk * half, wid)
        twin = swap_cores(halves, n_latent)
        for i, m in enumerate(ms):
            errors[m] = (halves[i], twin[i])

    errors = {}

    def columns(value, at):
        return lax.dynamic_slice_in_dim(value, (token ^ at) * wid, wid, 1)

    def own_rows(value, of_twin):
        at = 1 - core if of_twin else core
        return lax.dynamic_slice_in_dim(value, at * half, half, 0)

    res = jnp.concatenate([own_rows(res, False), own_rows(res, True)], axis=0)
    cols_a = exchange(jnp.stack([columns(res, side_a), columns(res, 2)]), "token", SIDE_A)
    cols_b = exchange(jnp.stack([columns(res, side_b), cols_a[1]]), "token", SIDE_B)
    cols = (columns(res, 0), cols_b[0], cols_a[0], cols_b[1])
    for ms in CHAINS:
        chain(ms)

    def outer(left, right):
        return lax.dot_general(left, right, (((0,), (0,)), ((), ())), preferred_element_type=F32)

    order_m = [m for ms in CHAINS for m in ms]
    early, late = [], []
    for h in range(2):
        d_lat = None
        for m in order_m:
            prod = lax.dot_general(
                errors[m][h], weight[m], (((1,), (1,)), ((), ())), preferred_element_type=F32
            )
            d_lat = prod if d_lat is None else d_lat + prod
        d_lat = d_lat.astype(BF16).reshape(n_token, half, -1)
        got = exchange(lax.dynamic_slice_in_dim(d_lat, 1 + core, 2, 0), "token", SIDE_A)
        mine = lax.dynamic_index_in_dim(got, core, 0, keepdims=False)
        other = lax.dynamic_index_in_dim(got, 1 - core, 0, keepdims=False)
        pass_on = lax.dynamic_index_in_dim(d_lat, side_b, 0, keepdims=False)
        pass_on = (pass_on.astype(F32) + other.astype(F32)).astype(BF16)
        d_total = d_lat[0].astype(F32) + mine.astype(F32)
        d_total = d_total + exchange(pass_on, "token", SIDE_B).astype(F32)
        d_pre = (d_total * gelu_slope(own_rows(preact, h == 1))).astype(BF16)
        near = exchange(d_pre, "token", SIDE_B)
        far = exchange(jnp.stack([d_pre, near]), "token", SIDE_A)
        span = slice(h * half, (h + 1) * half)
        early += [(cols[0][span], d_pre), (cols[1][span], near)]
        late += [(cols[2][span], far[0]), (cols[3][span], far[1])]
    enc_total = None
    for terms in (early, late):
        prod = outer(*(jnp.concatenate(side, axis=0) for side in zip(*terms)))
        enc_total = prod if enc_total is None else enc_total + prod
    grad_enc = enc_total.astype(BF16)

    lat_all = jnp.concatenate([lat[k] for k in ks], axis=0)
    grads = []
    for m in range(layers):
        err = jnp.stack(by_core(*(v.reshape(n_token, half, wid) for v in errors[m])), axis=1)
        grads.append(outer(lat_all, err.reshape(tokens_all, wid)).astype(BF16))

    return (jnp.stack(grads)[None], grad_enc[None])


def solution(mesh):
    placed = (
        P("layer", "token", None),
        P("layer", None, "latent"),
        P("layer", "latent"),
        P("layer", None, "latent", "token"),
        P("layer", "token"),
        P("layer", "latent", "token"),
    )
    return jax.shard_map(
        body,
        mesh=mesh,
        in_specs=placed,
        out_specs=(P("layer", None, "latent", "token"), P("layer", "token", "latent")),
        check_vma=False,
    )
```

profile of v0, /device:TPU:0, one launch (start us, length us, event | category | flops | bytes accessed | tf_op | source)
XLA Modules:
  0.0 169.0 jit_solution(2274233960495132335)
XLA Ops:
  0.6 4.9 %multiply_convert_fusion = (bf16[192,1024]{1,0:T(8,128)(2,1)S(1)}, f32[192,1024]{1,0:T(8,128)}) fusion(f32[1024]{0:T(1024)} %bitcast.400, bf16[1,2560,1024]{2,1,0:T(8,128)(2,1)} %param.11, bf16[1,192,2560]{2,1,0:T(8,128)(2,1)} %param.10), kind=kOutput, calls=%fused_computation.126 | convolution fusion | flops 1007812608 | bytes 7409664 | tf_op jit(solution)/shard_map/dot_general | solution.py:75
  5.5 3.1 %collective-permute-start = (bf16[192,1024]{1,0:T(8,128)(2,1)S(1)}, bf16[192,1024]{1,0:T(8,128)(2,1)S(1)}, u32[]{:S(2)}, u32[]{:S(2)}) collective-permute-start(bf16[192,1024]{1,0:T(8,128)(2,1)S(1)} %get-tuple-element.71), channel_id=1, source_target_pairs={{0,3},{1,2},{2,1},{3,0},{4,5},{5,4},{6,7},{7,6},{8,11},{9,10},{10,... | collective-permute-start | bytes 1179656 | tf_op jit(solution)/shard_map/ppermute | solution.py:45
  8.7 1.8 %fusion.54 = bf16[192,640]{1,0:T(8,128)(2,1)S(1)} fusion(bf16[192,1024]{1,0:T(8,128)(2,1)S(1)} %get-tuple-element.71, bf16[1,4,1024,640]{3,2,1,0:T(8,128)(2,1)} %param.13), kind=kOutput, calls=%fused_computation.75 | convolution fusion | flops 251781120 | bytes 1949696 | tf_op jit(solution)/shard_map/dot_general | solution.py:88
  10.5 1.8 %fusion.51 = bf16[192,640]{1,0:T(8,128)(2,1)S(1)} fusion(bf16[192,1024]{1,0:T(8,128)(2,1)S(1)} %get-tuple-element.71, bf16[1,4,1024,640]{3,2,1,0:T(8,128)(2,1)} %param.13), kind=kOutput, calls=%fused_computation.74 | convolution fusion | flops 251781120 | bytes 1949696 | tf_op jit(solution)/shard_map/dot_general | solution.py:88
  12.3 2.2 %collective-permute-done = bf16[192,1024]{1,0:T(8,128)(2,1)S(1)} collective-permute-done((bf16[192,1024]{1,0:T(8,128)(2,1)S(1)}, bf16[192,1024]{1,0:T(8,128)(2,1)S(1)}, u32[]{:S(2)}, u32[]{:S(2)}) %collective-permute-start) | collective-permute-done | bytes 393248 | tf_op jit(solution)/shard_map/ppermute | solution.py:45
  15.2 2.0 %fusion.48 = bf16[192,640]{1,0:T(8,128)(2,1)S(1)} fusion(bf16[192,1024]{1,0:T(8,128)(2,1)S(1)} %get-tuple-element.71, bf16[1,4,1024,640]{3,2,1,0:T(8,128)(2,1)} %param.13), kind=kOutput, calls=%fused_computation.73 | convolution fusion | flops 251781120 | bytes 1949696 | tf_op jit(solution)/shard_map/dot_general | solution.py:88
  17.2 1.8 %fusion.45 = bf16[192,640]{1,0:T(8,128)(2,1)S(1)} fusion(bf16[192,1024]{1,0:T(8,128)(2,1)S(1)} %get-tuple-element.71, bf16[1,4,1024,640]{3,2,1,0:T(8,128)(2,1)} %param.13), kind=kOutput, calls=%fused_computation.72 | convolution fusion | flops 251781120 | bytes 1949696 | tf_op jit(solution)/shard_map/dot_general | solution.py:88
  19.0 7.7 %collective-permute-done.1 = bf16[2,192,1024]{2,1,0:T(8,128)(2,1)S(1)} collective-permute-done((bf16[2,192,1024]{2,1,0:T(8,128)(2,1)S(1)}, bf16[2,192,1024]{2,1,0:T(8,128)(2,1)S(1)}, u32[]{:S(2)}, u32[]{:S(2)}) %collective-permute-start.1) | collective-permute-done | bytes 786464 | tf_op jit(solution)/shard_map/ppermute | solution.py:45
  26.8 1.1 convolution_convert_fusion.4
  27.9 1.1 convolution_convert_fusion.5
  30.1 1.1 convolution_convert_fusion.7
  35.9 1.3 dynamic-slice_bitcast_fusion
  38.3 2.5 %fusion.7 = (bf16[2,4,96,640]{3,2,1,0:T(8,128)(2,1)S(1)}, bf16[2,4,96,640]{3,2,1,0:T(8,128)(2,1)S(1)}) fusion(bf16[2,4,96,640]{3,2,1,0:T(8,128)(2,1)} %collective-permute-done.2, s32[]{:T(128)S(6)} %select_n.228, bf16[1,4,2,96,640]{4,3,1,0,2:T(8,128)(2,1)S(1)} %copy-done.2, bf16[1,4,2,96,640]{4,3,1,0,2:T(8,128)(2,1)S(1)} %maximum_bitcast_fusion.2, ...), kind=kLoop, calls=%fused_computation.19 | loop fusion | flops 7864320 | bytes 8110104 | tf_op jit(solution)/shard_map/convert_element_type | solution.py:107
  41.8 2.0 %collective-permute-start.3 = (bf16[2,2,4,24,640]{4,3,2,1,0:T(8,128)(2,1)}, bf16[2,2,4,24,640]{4,3,2,1,0:T(8,128)(2,1)}, u32[]{:S(2)}, u32[]{:S(2)}) collective-permute-start(bf16[2,2,4,24,640]{4,3,2,1,0:T(8,128)(2,1)} %pad_maximum_fusion.7), channel_id=1, source_target_pairs={{0,8},{4,28},{8,0},{12,20},{16,24},{20,12},{24,16},{28,4},{1,9},{5... | collective-permute-start | bytes 1474568 | tf_op jit(solution)/shard_map/ppermute | solution.py:45
  46.2 4.8 %collective-permute-done.3 = bf16[2,2,4,24,640]{4,3,2,1,0:T(8,128)(2,1)} collective-permute-done((bf16[2,2,4,24,640]{4,3,2,1,0:T(8,128)(2,1)}, bf16[2,2,4,24,640]{4,3,2,1,0:T(8,128)(2,1)}, u32[]{:S(2)}, u32[]{:S(2)}) %collective-permute-start.3) | collective-permute-done | bytes 491552 | tf_op jit(solution)/shard_map/ppermute | solution.py:45
  51.0 1.7 %fusion.120 = bf16[2,4,24,640]{3,2,1,0:T(8,128)(2,1)} fusion(bf16[2,2,4,24,640]{4,3,2,1,0:T(8,128)(2,1)} %collective-permute-done.3, bf16[2,4,4,24,640]{4,3,2,1,0:T(8,128)(2,1)S(1)} %bitcast.359, s32[]{:T(128)S(6)} %select_n.236), kind=kLoop, calls=%fused_computation.164 | loop fusion | flops 491520 | bytes 737284 | tf_op jit(solution)/shard_map/convert_element_type | solution.py:113
  52.7 4.1 %collective-permute-start.4 = (bf16[2,4,24,640]{3,2,1,0:T(8,128)(2,1)}, bf16[2,4,24,640]{3,2,1,0:T(8,128)(2,1)}, u32[]{:S(2)}, u32[]{:S(2)}) collective-permute-start(bf16[2,4,24,640]{3,2,1,0:T(8,128)(2,1)} %fusion.120), channel_id=1, source_target_pairs={{0,24},{4,12},{8,16},{12,4},{16,8},{20,28},{24,0},{28,20},{1,25},{... | collective-permute-start | bytes 737288 | tf_op jit(solution)/shard_map/ppermute | solution.py:45
  57.7 3.1 %collective-permute-start.12 = (bf16[2,4,24,640]{3,2,1,0:T(8,128)(2,1)S(1)}, bf16[2,4,24,640]{3,2,1,0:T(8,128)(2,1)S(1)}, u32[]{:S(2)}, u32[]{:S(2)}) collective-permute-start(bf16[2,4,24,640]{3,2,1,0:T(8,128)(2,1)S(1)} %fusion.117), channel_id=1, source_target_pairs={{0,24},{4,12},{8,16},{12,4},{16,8},{20,28},{24,0},{28,20},{1,25},{... | collective-permute-start | bytes 737288 | tf_op jit(solution)/shard_map/ppermute | solution.py:45
  60.8 1.9 %collective-permute-done.4 = bf16[2,4,24,640]{3,2,1,0:T(8,128)(2,1)} collective-permute-done((bf16[2,4,24,640]{3,2,1,0:T(8,128)(2,1)}, bf16[2,4,24,640]{3,2,1,0:T(8,128)(2,1)}, u32[]{:S(2)}, u32[]{:S(2)}) %collective-permute-start.4) | collective-permute-done | bytes 245792 | tf_op jit(solution)/shard_map/ppermute | solution.py:45
  62.7 1.2 fusion.122
  63.9 1.6 collective-permute-start.5
  65.6 1.7 %collective-permute-start.19 = (bf16[2,192,640]{2,1,0:T(8,128)(2,1)S(1)}, bf16[2,192,640]{2,1,0:T(8,128)(2,1)S(1)}, u32[]{:S(2)}, u32[]{:S(2)}) collective-permute-start(bf16[2,192,640]{2,1,0:T(8,128)(2,1)S(1)} %pad_maximum_fusion.12), channel_id=1, source_target_pairs={{0,3},{1,2},{2,1},{3,0},{4,5},{5,4},{6,7},{7,6},{8,11},{9,10},{10,... | collective-permute-start | bytes 1474568 | tf_op jit(solution)/shard_map/ppermute | solution.py:45
  67.3 1.6 collective-permute-done.5
  68.9 2.8 %collective-permute-start.6 = (bf16[1,4,24,640]{3,2,1,0:T(8,128)(2,1)S(1)}, bf16[1,4,24,640]{3,2,1,0:T(8,128)(2,1)S(1)}, u32[]{:S(2)}, u32[]{:S(2)}) collective-permute-start(bf16[1,4,24,640]{3,2,1,0:T(8,128)(2,1)S(1)} %add_convert_fusion.6), channel_id=1, source_target_pairs={{0,96},{32,64},{64,32},{96,0},{4,36},{36,4},{68,100},{100,68},{8,1... | collective-permute-start | bytes 368648 | tf_op jit(solution)/shard_map/ppermute | solution.py:45
  72.2 4.1 %collective-permute-done.6 = bf16[1,4,24,640]{3,2,1,0:T(8,128)(2,1)S(1)} collective-permute-done((bf16[1,4,24,640]{3,2,1,0:T(8,128)(2,1)S(1)}, bf16[1,4,24,640]{3,2,1,0:T(8,128)(2,1)S(1)}, u32[]{:S(2)}, u32[]{:S(2)}) %collective-permute-start.6) | collective-permute-done | bytes 122912 | tf_op jit(solution)/shard_map/ppermute | solution.py:45
  76.5 1.4 collective-permute-start.7
  78.2 2.4 %collective-permute-start.14 = (bf16[2,4,24,640]{3,2,1,0:T(8,128)(2,1)S(1)}, bf16[2,4,24,640]{3,2,1,0:T(8,128)(2,1)S(1)}, u32[]{:S(2)}, u32[]{:S(2)}) collective-permute-start(bf16[2,4,24,640]{3,2,1,0:T(8,128)(2,1)S(1)} %add_convert_fusion.3), channel_id=1, source_target_pairs={{0,96},{32,64},{64,32},{96,0},{4,36},{36,4},{68,100},{100,68},{8,1... | collective-permute-start | bytes 737288 | tf_op jit(solution)/shard_map/ppermute | solution.py:45
  81.0 4.7 %collective-permute-done.14 = bf16[2,4,24,640]{3,2,1,0:T(8,128)(2,1)S(1)} collective-permute-done((bf16[2,4,24,640]{3,2,1,0:T(8,128)(2,1)S(1)}, bf16[2,4,24,640]{3,2,1,0:T(8,128)(2,1)S(1)}, u32[]{:S(2)}, u32[]{:S(2)}) %collective-permute-start.14) | collective-permute-done | bytes 245792 | tf_op jit(solution)/shard_map/ppermute | solution.py:45
  86.0 2.1 %collective-permute-start.15 = (bf16[2,4,24,640]{3,2,1,0:T(8,128)(2,1)S(1)}, bf16[2,4,24,640]{3,2,1,0:T(8,128)(2,1)S(1)}, u32[]{:S(2)}, u32[]{:S(2)}) collective-permute-start(bf16[2,4,24,640]{3,2,1,0:T(8,128)(2,1)S(1)} %get-tuple-element.3), channel_id=1, source_target_pairs={{0,24},{4,12},{8,16},{12,4},{16,8},{20,28},{24,0},{28,20},{1,25},{... | collective-permute-start | bytes 737288 | tf_op jit(solution)/shard_map/ppermute | solution.py:45
  88.3 7.8 %collective-permute-done.15 = bf16[2,4,24,640]{3,2,1,0:T(8,128)(2,1)S(1)} collective-permute-done((bf16[2,4,24,640]{3,2,1,0:T(8,128)(2,1)S(1)}, bf16[2,4,24,640]{3,2,1,0:T(8,128)(2,1)S(1)}, u32[]{:S(2)}, u32[]{:S(2)}) %collective-permute-start.15) | collective-permute-done | bytes 245792 | tf_op jit(solution)/shard_map/ppermute | solution.py:45
  98.1 6.9 %collective-permute-done.16 = bf16[2,2,4,24,640]{4,3,2,1,0:T(8,128)(2,1)S(1)} collective-permute-done((bf16[2,2,4,24,640]{4,3,2,1,0:T(8,128)(2,1)S(1)}, bf16[2,2,4,24,640]{4,3,2,1,0:T(8,128)(2,1)S(1)}, u32[]{:S(2)}, u32[]{:S(2)}) %collective-permute-start.16) | collective-permute-done | bytes 491552 | tf_op jit(solution)/shard_map/ppermute | solution.py:45
  108.1 9.6 %collective-permute-done.20 = bf16[2,96,1024]{2,1,0:T(8,128)(2,1)S(1)} collective-permute-done((bf16[2,96,1024]{2,1,0:T(8,128)(2,1)S(1)}, bf16[2,96,1024]{2,1,0:T(8,128)(2,1)S(1)}, u32[]{:S(2)}, u32[]{:S(2)}) %collective-permute-start.20) | collective-permute-done | bytes 393248 | tf_op jit(solution)/shard_map/ppermute | solution.py:45
  117.7 3.0 %collective-permute-start.21 = (bf16[96,1024]{1,0:T(8,128)(2,1)S(1)}, bf16[96,1024]{1,0:T(8,128)(2,1)S(1)}, u32[]{:S(2)}, u32[]{:S(2)}) collective-permute-start(bf16[96,1024]{1,0:T(8,128)(2,1)S(1)} %fusion.154), channel_id=1, source_target_pairs={{0,3},{1,2},{2,1},{3,0},{4,5},{5,4},{6,7},{7,6},{8,11},{9,10},{10,... | collective-permute-start | bytes 589832 | tf_op jit(solution)/shard_map/ppermute | solution.py:45
  122.9 1.4 fusion.9
  124.4 1.4 fusion.10
  129.2 8.0 %collective-permute-done.23 = bf16[2,96,1024]{2,1,0:T(8,128)(2,1)S(1)} collective-permute-done((bf16[2,96,1024]{2,1,0:T(8,128)(2,1)S(1)}, bf16[2,96,1024]{2,1,0:T(8,128)(2,1)S(1)}, u32[]{:S(2)}, u32[]{:S(2)}) %collective-permute-start.23) | collective-permute-done | bytes 393248 | tf_op jit(solution)/shard_map/ppermute | solution.py:45
  137.2 1.7 collective-permute-start.24
  138.9 1.4 fusion.11
  140.4 4.0 %collective-permute-done.24 = bf16[96,1024]{1,0:T(8,128)(2,1)S(1)} collective-permute-done((bf16[96,1024]{1,0:T(8,128)(2,1)S(1)}, bf16[96,1024]{1,0:T(8,128)(2,1)S(1)}, u32[]{:S(2)}, u32[]{:S(2)}) %collective-permute-start.24) | collective-permute-done | bytes 196640 | tf_op jit(solution)/shard_map/ppermute | solution.py:45
  144.9 1.5 collective-permute-start.22
  146.3 1.9 %collective-permute-start.25 = (bf16[96,1024]{1,0:T(8,128)(2,1)S(1)}, bf16[96,1024]{1,0:T(8,128)(2,1)S(1)}, u32[]{:S(2)}, u32[]{:S(2)}) collective-permute-start(bf16[96,1024]{1,0:T(8,128)(2,1)S(1)} %get-tuple-element.33), channel_id=1, source_target_pairs={{0,3},{1,2},{2,1},{3,0},{4,5},{5,4},{6,7},{7,6},{8,11},{9,10},{10,... | collective-permute-start | bytes 589832 | tf_op jit(solution)/shard_map/ppermute | solution.py:45
  148.2 1.4 fusion.12
  149.7 4.3 %collective-permute-done.22 = bf16[96,1024]{1,0:T(8,128)(2,1)S(1)} collective-permute-done((bf16[96,1024]{1,0:T(8,128)(2,1)S(1)}, bf16[96,1024]{1,0:T(8,128)(2,1)S(1)}, u32[]{:S(2)}, u32[]{:S(2)}) %collective-permute-start.22) | collective-permute-done | bytes 196640 | tf_op jit(solution)/shard_map/ppermute | solution.py:45
  154.1 2.8 %collective-permute-done.25 = bf16[96,1024]{1,0:T(8,128)(2,1)S(1)} collective-permute-done((bf16[96,1024]{1,0:T(8,128)(2,1)S(1)}, bf16[96,1024]{1,0:T(8,128)(2,1)S(1)}, u32[]{:S(2)}, u32[]{:S(2)}) %collective-permute-start.25) | collective-permute-done | bytes 196640 | tf_op jit(solution)/shard_map/ppermute | solution.py:45
  157.0 3.0 %maximum_bitcast_fusion = bf16[1,4,1024,640]{3,2,1,0:T(8,128)(2,1)} fusion(bf16[1,1024,640]{2,1,0:T(8,128)(2,1)S(1)} %fusion.12, bf16[1,1024,640]{2,1,0:T(8,128)(2,1)S(1)} %fusion.11, bf16[1,1024,640]{2,1,0:T(8,128)(2,1)S(1)} %fusion.10, bf16[1,1024,640]{2,1,0:T(8,128)(2,1)S(1)} %fusion.9), kind=kLoop, calls=%fused_computation | loop fusion | flops 7864320 | bytes 10485760 | tf_op jit(solution)/shard_map/broadcast_in_dim | solution.py:189
  159.9 1.9 %collective-permute-done.26 = bf16[2,96,1024]{2,1,0:T(8,128)(2,1)S(1)} collective-permute-done((bf16[2,96,1024]{2,1,0:T(8,128)(2,1)S(1)}, bf16[2,96,1024]{2,1,0:T(8,128)(2,1)S(1)}, u32[]{:S(2)}, u32[]{:S(2)}) %collective-permute-start.26) | collective-permute-done | bytes 393248 | tf_op jit(solution)/shard_map/ppermute | solution.py:45
  161.9 4.2 %collective-permute-done.27 = bf16[2,96,1024]{2,1,0:T(8,128)(2,1)S(1)} collective-permute-done((bf16[2,96,1024]{2,1,0:T(8,128)(2,1)S(1)}, bf16[2,96,1024]{2,1,0:T(8,128)(2,1)S(1)}, u32[]{:S(2)}, u32[]{:S(2)}) %collective-permute-start.27) | collective-permute-done | bytes 393248 | tf_op jit(solution)/shard_map/ppermute | solution.py:45
  167.1 2.0 %fusion.8 = bf16[1,640,1024]{2,1,0:T(8,128)(2,1)} fusion(f32[640,1024]{1,0:T(8,128)S(1)} %fusion.89, bf16[96,1024]{1,0:T(8,128)(2,1)S(1)} %collective-permute-done.25, bf16[96,1024]{1,0:T(8,128)(2,1)S(1)} %get-tuple-element.33, bf16[96,1024]{1,0:T(8,128)(2,1)S(1)} %collective-permute-done.22, bf16[96,1024]{1,0:T(8,128)(2,1)S(1)} %get-tuple-element.32, ...), kind=kOutput, calls=%fused_computation.27 | convolution fusion | flops 509739008 | bytes 5210112 | tf_op jit(solution)/shard_map/dot_general | solution.py:152
  (157 shorter events, 25.5 us)
Async XLA Ops:
  5.5 11.6 %copy-start.10 = (bf16[192,1024]{1,0:T(8,128)(2,1)}, bf16[192,1024]{1,0:T(8,128)(2,1)S(1)}, u32[]{:S(2)}) copy-start(bf16[192,1024]{1,0:T(8,128)(2,1)S(1)} %get-tuple-element.71) | copy-start | bytes 1179652
  5.5 9.0 %collective-permute-start = (bf16[192,1024]{1,0:T(8,128)(2,1)S(1)}, bf16[192,1024]{1,0:T(8,128)(2,1)S(1)}, u32[]{:S(2)}, u32[]{:S(2)}) collective-permute-start(bf16[192,1024]{1,0:T(8,128)(2,1)S(1)} %get-tuple-element.71), channel_id=1, source_target_pairs={{0,3},{1,2},{2,1},{3,0},{4,5},{5,4},{6,7},{7,6},{8,11},{9,10},{10,... | collective-permute-start | bytes 1179656 | tf_op jit(solution)/shard_map/ppermute | solution.py:45
  10.5 4.7 %copy-start.20 = (s32[2]{0:T(128)S(1)}, s32[2]{0:T(128)}, u32[]{:S(2)}) copy-start(s32[2]{0:T(128)} %constant.145.clone) | copy-start | bytes 28
  14.6 12.1 %collective-permute-start.1 = (bf16[2,192,1024]{2,1,0:T(8,128)(2,1)S(1)}, bf16[2,192,1024]{2,1,0:T(8,128)(2,1)S(1)}, u32[]{:S(2)}, u32[]{:S(2)}) collective-permute-start(bf16[2,192,1024]{2,1,0:T(8,128)(2,1)S(1)} %pad_maximum_fusion.6), channel_id=1, source_target_pairs={{0,1},{1,0},{2,3},{3,2},{4,7},{5,6},{6,5},{7,4},{8,9},{9,8},{10,11... | collective-permute-start | bytes 2359304 | tf_op jit(solution)/shard_map/ppermute | solution.py:45
  15.2 11.6 %copy-start = (bf16[1,4,1024,640]{3,2,1,0:T(8,128)(2,1)S(1)}, bf16[1,4,1024,640]{3,2,1,0:T(8,128)(2,1)}, u32[]{:S(2)}) copy-start(bf16[1,4,1024,640]{3,2,1,0:T(8,128)(2,1)} %param.13) | copy-start | bytes 15728644
  26.7 3.4 %copy-start.8 = (bf16[192,1024]{1,0:T(8,128)(2,1)}, bf16[192,1024]{1,0:T(8,128)(2,1)S(1)}, u32[]{:S(2)}) copy-start(bf16[192,1024]{1,0:T(8,128)(2,1)S(1)} %slice_bitcast_fusion) | copy-start | bytes 1179652
  26.8 3.3 %copy-start.12 = (bf16[192,1024]{1,0:T(8,128)(2,1)}, bf16[192,1024]{1,0:T(8,128)(2,1)S(1)}, u32[]{:S(2)}) copy-start(bf16[192,1024]{1,0:T(8,128)(2,1)S(1)} %get-tuple-element.4) | copy-start | bytes 1179652
  26.8 3.3 %copy-start.14 = (bf16[192,1024]{1,0:T(8,128)(2,1)}, bf16[192,1024]{1,0:T(8,128)(2,1)S(1)}, u32[]{:S(2)}) copy-start(bf16[192,1024]{1,0:T(8,128)(2,1)S(1)} %get-tuple-element.5) | copy-start | bytes 1179652
  32.8 4.5 %collective-permute-start.10 = (bf16[2,4,96,640]{3,2,1,0:T(8,128)(2,1)}, bf16[2,4,96,640]{3,2,1,0:T(8,128)(2,1)}, u32[]{:S(2)}, u32[]{:S(2)}) collective-permute-start(bf16[2,4,96,640]{3,2,1,0:T(8,128)(2,1)} %fusion.58), channel_id=1, source_target_pairs={{0,4},{4,0},{8,12},{12,8},{16,20},{20,16},{24,28},{28,24},{1,5},{5... | collective-permute-start | bytes 2949128 | tf_op jit(solution)/shard_map/ppermute | solution.py:28
  34.2 1.6 copy-start.19
  34.2 1.7 %copy-start.16 = (bf16[1,96,640]{2,1,0:T(8,128)(2,1)S(1)}, bf16[1,96,640]{2,1,0:T(8,128)(2,1)}, u32[]{:S(2)}) copy-start(bf16[1,96,640]{2,1,0:T(8,128)(2,1)} %param.15) | copy-start | bytes 368644
  35.2 3.0 %collective-permute-start.2 = (bf16[2,4,96,640]{3,2,1,0:T(8,128)(2,1)}, bf16[2,4,96,640]{3,2,1,0:T(8,128)(2,1)}, u32[]{:S(2)}, u32[]{:S(2)}) collective-permute-start(bf16[2,4,96,640]{3,2,1,0:T(8,128)(2,1)} %fusion.62), channel_id=1, source_target_pairs={{0,4},{4,0},{8,12},{12,8},{16,20},{20,16},{24,28},{28,24},{1,5},{5... | collective-permute-start | bytes 2949128 | tf_op jit(solution)/shard_map/ppermute | solution.py:28
  35.8 2.5 %copy-start.2 = (bf16[1,4,2,96,640]{4,3,1,0,2:T(8,128)(2,1)S(1)}, bf16[1,4,2,96,640]{4,3,1,0,2:T(8,128)(2,1)}, u32[]{:S(2)}) copy-start(bf16[1,4,2,96,640]{4,3,1,0,2:T(8,128)(2,1)} %copy-done.1) | copy-start | bytes 2949124
  40.8 3.2 %copy-start.5 = (bf16[2,4,96,640]{3,2,1,0:T(8,128)(2,1)}, bf16[2,4,96,640]{3,2,1,0:T(8,128)(2,1)S(1)}, u32[]{:S(2)}) copy-start(bf16[2,4,96,640]{3,2,1,0:T(8,128)(2,1)S(1)} %get-tuple-element.65) | copy-start | bytes 2949124
  40.8 4.4 %copy-start.3 = (bf16[2,4,96,640]{3,2,1,0:T(8,128)(2,1)}, bf16[2,4,96,640]{3,2,1,0:T(8,128)(2,1)S(1)}, u32[]{:S(2)}) copy-start(bf16[2,4,96,640]{3,2,1,0:T(8,128)(2,1)S(1)} %get-tuple-element.66) | copy-start | bytes 2949124
  41.8 9.2 %collective-permute-start.3 = (bf16[2,2,4,24,640]{4,3,2,1,0:T(8,128)(2,1)}, bf16[2,2,4,24,640]{4,3,2,1,0:T(8,128)(2,1)}, u32[]{:S(2)}, u32[]{:S(2)}) collective-permute-start(bf16[2,2,4,24,640]{4,3,2,1,0:T(8,128)(2,1)} %pad_maximum_fusion.7), channel_id=1, source_target_pairs={{0,8},{4,28},{8,0},{12,20},{16,24},{20,12},{24,16},{28,4},{1,9},{5... | collective-permute-start | bytes 1474568 | tf_op jit(solution)/shard_map/ppermute | solution.py:45
  44.0 7.0 %copy-start.6 = (bf16[2,4,96,640]{3,2,1,0:T(8,128)(2,1)S(1)}, bf16[2,4,96,640]{3,2,1,0:T(8,128)(2,1)}, u32[]{:S(2)}) copy-start(bf16[2,4,96,640]{3,2,1,0:T(8,128)(2,1)} %copy-done.5) | copy-start | bytes 2949124
  44.8 12.7 %collective-permute-start.18 = (bf16[2,192,640]{2,1,0:T(8,128)(2,1)}, bf16[2,192,640]{2,1,0:T(8,128)(2,1)S(1)}, u32[]{:S(2)}, u32[]{:S(2)}) collective-permute-start(bf16[2,192,640]{2,1,0:T(8,128)(2,1)} %pad_maximum_fusion.11), channel_id=1, source_target_pairs={{0,1},{1,0},{2,3},{3,2},{4,7},{5,6},{6,5},{7,4},{8,9},{9,8},{10,11... | collective-permute-start | bytes 1474568 | tf_op jit(solution)/shard_map/ppermute | solution.py:45
  45.3 12.3 %copy-start.4 = (bf16[2,4,96,640]{3,2,1,0:T(8,128)(2,1)S(1)}, bf16[2,4,96,640]{3,2,1,0:T(8,128)(2,1)}, u32[]{:S(2)}) copy-start(bf16[2,4,96,640]{3,2,1,0:T(8,128)(2,1)} %copy-done.3) | copy-start | bytes 2949124
  46.1 11.5 %collective-permute-start.11 = (bf16[2,2,4,24,640]{4,3,2,1,0:T(8,128)(2,1)}, bf16[2,2,4,24,640]{4,3,2,1,0:T(8,128)(2,1)S(1)}, u32[]{:S(2)}, u32[]{:S(2)}) collective-permute-start(bf16[2,2,4,24,640]{4,3,2,1,0:T(8,128)(2,1)} %pad_maximum_fusion.9), channel_id=1, source_target_pairs={{0,8},{4,28},{8,0},{12,20},{16,24},{20,12},{24,16},{28,4},{1,9},{5... | collective-permute-start | bytes 1474568 | tf_op jit(solution)/shard_map/ppermute | solution.py:45
  52.7 10.0 %collective-permute-start.4 = (bf16[2,4,24,640]{3,2,1,0:T(8,128)(2,1)}, bf16[2,4,24,640]{3,2,1,0:T(8,128)(2,1)}, u32[]{:S(2)}, u32[]{:S(2)}) collective-permute-start(bf16[2,4,24,640]{3,2,1,0:T(8,128)(2,1)} %fusion.120), channel_id=1, source_target_pairs={{0,24},{4,12},{8,16},{12,4},{16,8},{20,28},{24,0},{28,20},{1,25},{... | collective-permute-start | bytes 737288 | tf_op jit(solution)/shard_map/ppermute | solution.py:45
  57.7 14.1 %collective-permute-start.12 = (bf16[2,4,24,640]{3,2,1,0:T(8,128)(2,1)S(1)}, bf16[2,4,24,640]{3,2,1,0:T(8,128)(2,1)S(1)}, u32[]{:S(2)}, u32[]{:S(2)}) collective-permute-start(bf16[2,4,24,640]{3,2,1,0:T(8,128)(2,1)S(1)} %fusion.117), channel_id=1, source_target_pairs={{0,24},{4,12},{8,16},{12,4},{16,8},{20,28},{24,0},{28,20},{1,25},{... | collective-permute-start | bytes 737288 | tf_op jit(solution)/shard_map/ppermute | solution.py:45
  63.9 5.0 %collective-permute-start.5 = (bf16[1,4,24,640]{3,2,1,0:T(8,128)(2,1)S(1)}, bf16[1,4,24,640]{3,2,1,0:T(8,128)(2,1)S(1)}, u32[]{:S(2)}, u32[]{:S(2)}) collective-permute-start(bf16[1,4,24,640]{3,2,1,0:T(8,128)(2,1)S(1)} %get-tuple-element.60), channel_id=1, source_target_pairs={{0,32},{32,0},{64,96},{96,64},{4,100},{36,68},{68,36},{100,4},{8,4... | collective-permute-start | bytes 368648 | tf_op jit(solution)/shard_map/ppermute | solution.py:45
  65.6 42.3 %collective-permute-start.19 = (bf16[2,192,640]{2,1,0:T(8,128)(2,1)S(1)}, bf16[2,192,640]{2,1,0:T(8,128)(2,1)S(1)}, u32[]{:S(2)}, u32[]{:S(2)}) collective-permute-start(bf16[2,192,640]{2,1,0:T(8,128)(2,1)S(1)} %pad_maximum_fusion.12), channel_id=1, source_target_pairs={{0,3},{1,2},{2,1},{3,0},{4,5},{5,4},{6,7},{7,6},{8,11},{9,10},{10,... | collective-permute-start | bytes 1474568 | tf_op jit(solution)/shard_map/ppermute | solution.py:45
  68.9 28.4 %slice-start = ((s8[5242880]{0:T(1024)(128)(4,1)}), s8[4194304]{0:T(1024)(128)(4,1)S(1)}, s32[]{:S(2)}) async-start(s8[5242880]{0:T(1024)(128)(4,1)} %bitcast.349), calls=%async_computation | async-start | bytes 8388608
  68.9 7.4 %collective-permute-start.6 = (bf16[1,4,24,640]{3,2,1,0:T(8,128)(2,1)S(1)}, bf16[1,4,24,640]{3,2,1,0:T(8,128)(2,1)S(1)}, u32[]{:S(2)}, u32[]{:S(2)}) collective-permute-start(bf16[1,4,24,640]{3,2,1,0:T(8,128)(2,1)S(1)} %add_convert_fusion.6), channel_id=1, source_target_pairs={{0,96},{32,64},{64,32},{96,0},{4,36},{36,4},{68,100},{100,68},{8,1... | collective-permute-start | bytes 368648 | tf_op jit(solution)/shard_map/ppermute | solution.py:45
  71.9 6.3 %collective-permute-start.13 = (bf16[2,4,24,640]{3,2,1,0:T(8,128)(2,1)S(1)}, bf16[2,4,24,640]{3,2,1,0:T(8,128)(2,1)S(1)}, u32[]{:S(2)}, u32[]{:S(2)}) collective-permute-start(bf16[2,4,24,640]{3,2,1,0:T(8,128)(2,1)S(1)} %fusion.119), channel_id=1, source_target_pairs={{0,32},{32,0},{64,96},{96,64},{4,100},{36,68},{68,36},{100,4},{8,4... | collective-permute-start | bytes 737288 | tf_op jit(solution)/shard_map/ppermute | solution.py:45
  76.5 11.6 %collective-permute-start.7 = (bf16[2,4,24,640]{3,2,1,0:T(8,128)(2,1)S(1)}, bf16[2,4,24,640]{3,2,1,0:T(8,128)(2,1)S(1)}, u32[]{:S(2)}, u32[]{:S(2)}) collective-permute-start(bf16[2,4,24,640]{3,2,1,0:T(8,128)(2,1)S(1)} %fusion.100), channel_id=1, source_target_pairs={{0,24},{4,12},{8,16},{12,4},{16,8},{20,28},{24,0},{28,20},{1,25},{... | collective-permute-start | bytes 737288 | tf_op jit(solution)/shard_map/ppermute | solution.py:45
  78.2 7.5 %collective-permute-start.14 = (bf16[2,4,24,640]{3,2,1,0:T(8,128)(2,1)S(1)}, bf16[2,4,24,640]{3,2,1,0:T(8,128)(2,1)S(1)}, u32[]{:S(2)}, u32[]{:S(2)}) collective-permute-start(bf16[2,4,24,640]{3,2,1,0:T(8,128)(2,1)S(1)} %add_convert_fusion.3), channel_id=1, source_target_pairs={{0,96},{32,64},{64,32},{96,0},{4,36},{36,4},{68,100},{100,68},{8,1... | collective-permute-start | bytes 737288 | tf_op jit(solution)/shard_map/ppermute | solution.py:45
  81.0 16.3 %slice-start.1 = ((s8[5242880]{0:T(1024)(128)(4,1)}), s8[1048576]{0:T(1024)(128)(4,1)S(1)}, s32[]{:S(2)}) async-start(s8[5242880]{0:T(1024)(128)(4,1)} %bitcast.349), calls=%async_computation.1 | async-start | bytes 2097152
  86.0 10.1 %collective-permute-start.15 = (bf16[2,4,24,640]{3,2,1,0:T(8,128)(2,1)S(1)}, bf16[2,4,24,640]{3,2,1,0:T(8,128)(2,1)S(1)}, u32[]{:S(2)}, u32[]{:S(2)}) collective-permute-start(bf16[2,4,24,640]{3,2,1,0:T(8,128)(2,1)S(1)} %get-tuple-element.3), channel_id=1, source_target_pairs={{0,24},{4,12},{8,16},{12,4},{16,8},{20,28},{24,0},{28,20},{1,25},{... | collective-permute-start | bytes 737288 | tf_op jit(solution)/shard_map/ppermute | solution.py:45
  88.1 8.9 %collective-permute-start.8 = (bf16[2,2,4,24,640]{4,3,2,1,0:T(8,128)(2,1)S(1)}, bf16[2,2,4,24,640]{4,3,2,1,0:T(8,128)(2,1)S(1)}, u32[]{:S(2)}, u32[]{:S(2)}) collective-permute-start(bf16[2,2,4,24,640]{4,3,2,1,0:T(8,128)(2,1)S(1)} %pad_maximum_fusion.8), channel_id=1, source_target_pairs={{0,8},{4,28},{8,0},{12,20},{16,24},{20,12},{24,16},{28,4},{1,9},{5... | collective-permute-start | bytes 1474568 | tf_op jit(solution)/shard_map/ppermute | solution.py:45
  96.1 8.9 %collective-permute-start.16 = (bf16[2,2,4,24,640]{4,3,2,1,0:T(8,128)(2,1)S(1)}, bf16[2,2,4,24,640]{4,3,2,1,0:T(8,128)(2,1)S(1)}, u32[]{:S(2)}, u32[]{:S(2)}) collective-permute-start(bf16[2,2,4,24,640]{4,3,2,1,0:T(8,128)(2,1)S(1)} %pad_maximum_fusion.10), channel_id=1, source_target_pairs={{0,8},{4,28},{8,0},{12,20},{16,24},{20,12},{24,16},{28,4},{1,9},{5... | collective-permute-start | bytes 1474568 | tf_op jit(solution)/shard_map/ppermute | solution.py:45
  97.1 23.7 %collective-permute-start.9 = (bf16[2,384,640]{2,1,0:T(8,128)(2,1)S(1)}, bf16[2,384,640]{2,1,0:T(8,128)(2,1)S(1)}, u32[]{:S(2)}, u32[]{:S(2)}) collective-permute-start(bf16[2,384,640]{2,1,0:T(8,128)(2,1)S(1)} %bitcast.362), channel_id=1, source_target_pairs={{0,4},{4,0},{8,12},{12,8},{16,20},{20,16},{24,28},{28,24},{1,5},{5... | collective-permute-start | bytes 2949128 | tf_op jit(solution)/shard_map/ppermute | solution.py:28
  107.7 10.0 %collective-permute-start.20 = (bf16[2,96,1024]{2,1,0:T(8,128)(2,1)S(1)}, bf16[2,96,1024]{2,1,0:T(8,128)(2,1)S(1)}, u32[]{:S(2)}, u32[]{:S(2)}) collective-permute-start(bf16[2,96,1024]{2,1,0:T(8,128)(2,1)S(1)} %constant_dynamic-slice_fusion.1), channel_id=1, source_target_pairs={{0,1},{1,0},{2,3},{3,2},{4,7},{5,6},{6,5},{7,4},{8,9},{9,8},{10,11... | collective-permute-start | bytes 1179656 | tf_op jit(solution)/shard_map/ppermute | solution.py:45
  108.0 17.9 %collective-permute-start.17 = (bf16[2,384,640]{2,1,0:T(8,128)(2,1)S(1)}, bf16[2,384,640]{2,1,0:T(8,128)(2,1)S(1)}, u32[]{:S(2)}, u32[]{:S(2)}) collective-permute-start(bf16[2,384,640]{2,1,0:T(8,128)(2,1)S(1)} %bitcast.361), channel_id=1, source_target_pairs={{0,4},{4,0},{8,12},{12,8},{16,20},{20,16},{24,28},{28,24},{1,5},{5... | collective-permute-start | bytes 2949128 | tf_op jit(solution)/shard_map/ppermute | solution.py:28
  117.7 22.6 %collective-permute-start.21 = (bf16[96,1024]{1,0:T(8,128)(2,1)S(1)}, bf16[96,1024]{1,0:T(8,128)(2,1)S(1)}, u32[]{:S(2)}, u32[]{:S(2)}) collective-permute-start(bf16[96,1024]{1,0:T(8,128)(2,1)S(1)} %fusion.154), channel_id=1, source_target_pairs={{0,3},{1,2},{2,1},{3,0},{4,5},{5,4},{6,7},{7,6},{8,11},{9,10},{10,... | collective-permute-start | bytes 589832 | tf_op jit(solution)/shard_map/ppermute | solution.py:45
  121.6 1.0 copy-start.9
  121.6 1.1 copy-start.11
  121.6 1.2 copy-start.13
  121.6 1.3 copy-start.15
  128.3 8.9 %collective-permute-start.23 = (bf16[2,96,1024]{2,1,0:T(8,128)(2,1)S(1)}, bf16[2,96,1024]{2,1,0:T(8,128)(2,1)S(1)}, u32[]{:S(2)}, u32[]{:S(2)}) collective-permute-start(bf16[2,96,1024]{2,1,0:T(8,128)(2,1)S(1)} %constant_dynamic-slice_fusion), channel_id=1, source_target_pairs={{0,1},{1,0},{2,3},{3,2},{4,7},{5,6},{6,5},{7,4},{8,9},{9,8},{10,11... | collective-permute-start | bytes 1179656 | tf_op jit(solution)/shard_map/ppermute | solution.py:45
  137.2 7.2 %collective-permute-start.24 = (bf16[96,1024]{1,0:T(8,128)(2,1)S(1)}, bf16[96,1024]{1,0:T(8,128)(2,1)S(1)}, u32[]{:S(2)}, u32[]{:S(2)}) collective-permute-start(bf16[96,1024]{1,0:T(8,128)(2,1)S(1)} %fusion.155), channel_id=1, source_target_pairs={{0,3},{1,2},{2,1},{3,0},{4,5},{5,4},{6,7},{7,6},{8,11},{9,10},{10,... | collective-permute-start | bytes 589832 | tf_op jit(solution)/shard_map/ppermute | solution.py:45
  138.9 5.5 %copy-start.7 = (f32[192,1024]{1,0:T(8,128)S(1)}, f32[192,1024]{1,0:T(8,128)}, u32[]{:S(2)}) copy-start(f32[192,1024]{1,0:T(8,128)} %get-tuple-element.72) | copy-start | bytes 2359300
  144.9 9.1 %collective-permute-start.22 = (bf16[96,1024]{1,0:T(8,128)(2,1)S(1)}, bf16[96,1024]{1,0:T(8,128)(2,1)S(1)}, u32[]{:S(2)}, u32[]{:S(2)}) collective-permute-start(bf16[96,1024]{1,0:T(8,128)(2,1)S(1)} %get-tuple-element.32), channel_id=1, source_target_pairs={{0,3},{1,2},{2,1},{3,0},{4,5},{5,4},{6,7},{7,6},{8,11},{9,10},{10,... | collective-permute-start | bytes 589832 | tf_op jit(solution)/shard_map/ppermute | solution.py:45
  146.3 10.5 %collective-permute-start.25 = (bf16[96,1024]{1,0:T(8,128)(2,1)S(1)}, bf16[96,1024]{1,0:T(8,128)(2,1)S(1)}, u32[]{:S(2)}, u32[]{:S(2)}) collective-permute-start(bf16[96,1024]{1,0:T(8,128)(2,1)S(1)} %get-tuple-element.33), channel_id=1, source_target_pairs={{0,3},{1,2},{2,1},{3,0},{4,5},{5,4},{6,7},{7,6},{8,11},{9,10},{10,... | collective-permute-start | bytes 589832 | tf_op jit(solution)/shard_map/ppermute | solution.py:45
  154.0 7.9 %collective-permute-start.26 = (bf16[2,96,1024]{2,1,0:T(8,128)(2,1)S(1)}, bf16[2,96,1024]{2,1,0:T(8,128)(2,1)S(1)}, u32[]{:S(2)}, u32[]{:S(2)}) collective-permute-start(bf16[2,96,1024]{2,1,0:T(8,128)(2,1)S(1)} %pad_maximum_fusion.13), channel_id=1, source_target_pairs={{0,1},{1,0},{2,3},{3,2},{4,7},{5,6},{6,5},{7,4},{8,9},{9,8},{10,11... | collective-permute-start | bytes 1179656 | tf_op jit(solution)/shard_map/ppermute | solution.py:45
  156.9 9.2 %collective-permute-start.27 = (bf16[2,96,1024]{2,1,0:T(8,128)(2,1)S(1)}, bf16[2,96,1024]{2,1,0:T(8,128)(2,1)S(1)}, u32[]{:S(2)}, u32[]{:S(2)}) collective-permute-start(bf16[2,96,1024]{2,1,0:T(8,128)(2,1)S(1)} %pad_maximum_fusion.14), channel_id=1, source_target_pairs={{0,1},{1,0},{2,3},{3,2},{4,7},{5,6},{6,5},{7,4},{8,9},{9,8},{10,11... | collective-permute-start | bytes 1179656 | tf_op jit(solution)/shard_map/ppermute | solution.py:45
  (3 other events, 2.8 us)
where the time goes:
time: 169 us
  waiting for transfers between devices  78.6 us (47%)
  starting transfers between devices  35.1 us (21%)
  matrix products  31.7 us (19%)
  other arithmetic  16.8 us (10%)
  local copies, waits for them, and re-layouts  5.33 us (3%)
    ppermute x24, waiting for transfers between devices, exchange(): return lax.ppermute(value, names, pairs)  77.6 us
    ppermute x24, starting transfers between devices, exchange(): return lax.ppermute(value, names, pairs)  34.4 us
    dot_general x8, matrix products, body(): prod = jnp.dot(lhs, weight[m], preferred_element_type=F32).astype(BF16)  11.7 us
    dot_general x6, matrix products, outer(): lax.dot_general(left, right, (((0,), (0,)), ((), ())), preferred_element_...  8.61 us
    dot_general x8, matrix products, body(): lax.dot_general(errors[m][h], weight[m], (((1,), (1,)), ((), ())), prefer...  6.44 us
    dot_general x1, matrix products, body(): jnp.dot(res, enc_weight[0], preferred_element_type=F32) + enc_bias[0]  4.91 us
  transfers between devices with their start and end apart: 28, of which 19 were waited for; matrix products, arithmetic and copies ran while one was open for 20% of the time, Pallas kernels for 0%

commit v1 on v0

--- a/solution.py
+++ b/solution.py
@@ -116,8 +116,11 @@
         summed = summed.astype(BF16)
         first = 1 if ms[0] == 0 else 0
         upper = summed[first:]
-        upper = (upper.astype(F32) + exchange(upper, "layer", SIDE_A).astype(F32)).astype(BF16)
-        error = upper.astype(F32) + exchange(upper, "layer", SIDE_B).astype(F32)
+        if max(ms) < 2:
+            error = upper.astype(F32) + exchange(upper, "layer", (1, 1)).astype(F32)
+        else:
+            upper = (upper.astype(F32) + exchange(upper, "layer", SIDE_A).astype(F32)).astype(BF16)
+            error = upper.astype(F32) + exchange(upper, "layer", SIDE_B).astype(F32)
         if first:
             error = jnp.concatenate([summed[:1].astype(F32), error])
         error = jnp.where(live, LOSS_SCALE / tokens_all * error, 0.0).astype(BF16)
@@ -151,7 +154,7 @@
     def outer(left, right):
         return lax.dot_general(left, right, (((0,), (0,)), ((), ())), preferred_element_type=F32)
 
-    order_m = [m for ms in CHAINS for m in ms]
+    order_m = [m for ms in CHAINS[::-1] for m in ms]
     early, late = [], []
     for h in range(2):
         d_lat = None

time: 169 us -> 167 us (0.988)
  the two profiles are of different devices: /device:TPU:0 before, /device:TPU:96 now
where the time goes in v1:
time: 167 us; the launch traced here: 166 us
  waiting for transfers between devices  81.1 us (49%)
  matrix products  35.3 us (21%)
  starting transfers between devices  31.6 us (19%)
  other arithmetic  12.5 us (7%)
  local copies, waits for them, and re-layouts  4.18 us (3%)
    ppermute x23, waiting for transfers between devices, exchange(): return lax.ppermute(value, names, pairs)  78.6 us
    ppermute x23, starting transfers between devices, exchange(): return lax.ppermute(value, names, pairs)  30.8 us
    dot_general x6, matrix products, outer(): lax.dot_general(left, right, (((0,), (0,)), ((), ())), preferred_element_...  12.6 us
    dot_general x8, matrix products, body(): prod = jnp.dot(lhs, weight[m], preferred_element_type=F32).astype(BF16)  11.3 us
    dot_general x8, matrix products, body(): lax.dot_general(errors[m][h], weight[m], (((1,), (1,)), ((), ())), prefer...  6.45 us
    dot_general x1, matrix products, body(): jnp.dot(res, enc_weight[0], preferred_element_type=F32) + enc_bias[0]  4.89 us
  transfers between devices with their start and end apart: 27, of which 20 were waited for; matrix products, arithmetic and copies ran while one was open for 26% of the time, Pallas kernels for 0%

profile of v1, /device:TPU:96, one launch (start us, length us, event | category | flops | bytes accessed | tf_op | source)
XLA Modules:
  0.0 166.3 jit_solution(170520103261943560)
XLA Ops:
  0.6 4.9 %multiply_convert_fusion = (bf16[192,1024]{1,0:T(8,128)(2,1)}, f32[192,1024]{1,0:T(8,128)S(1)}) fusion(f32[1024]{0:T(1024)} %bitcast.399, bf16[1,2560,1024]{2,1,0:T(8,128)(2,1)} %param.11, bf16[1,192,2560]{2,1,0:T(8,128)(2,1)} %param.10), kind=kOutput, calls=%fused_computation.126 | convolution fusion | flops 1007812608 | bytes 7409664 | tf_op jit(solution)/shard_map/dot_general | solution.py:75
  5.5 3.0 %collective-permute-start = (bf16[192,1024]{1,0:T(8,128)(2,1)}, bf16[192,1024]{1,0:T(8,128)(2,1)S(1)}, u32[]{:S(2)}, u32[]{:S(2)}) collective-permute-start(bf16[192,1024]{1,0:T(8,128)(2,1)} %get-tuple-element.71), channel_id=1, source_target_pairs={{0,3},{1,2},{2,1},{3,0},{4,5},{5,4},{6,7},{7,6},{8,11},{9,10},{10,... | collective-permute-start | bytes 1179656 | tf_op jit(solution)/shard_map/ppermute | solution.py:45
  9.8 2.1 %fusion.54 = bf16[192,640]{1,0:T(8,128)(2,1)S(1)} fusion(bf16[192,1024]{1,0:T(8,128)(2,1)} %get-tuple-element.71, bf16[1,4,1024,640]{3,2,1,0:T(8,128)(2,1)} %param.13), kind=kOutput, calls=%fused_computation.75 | convolution fusion | flops 251781120 | bytes 1949696 | tf_op jit(solution)/shard_map/dot_general | solution.py:88
  11.8 6.2 %collective-permute-done = bf16[192,1024]{1,0:T(8,128)(2,1)S(1)} collective-permute-done((bf16[192,1024]{1,0:T(8,128)(2,1)}, bf16[192,1024]{1,0:T(8,128)(2,1)S(1)}, u32[]{:S(2)}, u32[]{:S(2)}) %collective-permute-start) | collective-permute-done | bytes 393248 | tf_op jit(solution)/shard_map/ppermute | solution.py:45
  18.0 1.1 pad_maximum_fusion.6
  19.7 1.9 %fusion.51 = bf16[192,640]{1,0:T(8,128)(2,1)S(1)} fusion(bf16[192,1024]{1,0:T(8,128)(2,1)} %get-tuple-element.71, bf16[1,4,1024,640]{3,2,1,0:T(8,128)(2,1)} %param.13), kind=kOutput, calls=%fused_computation.74 | convolution fusion | flops 251781120 | bytes 1949696 | tf_op jit(solution)/shard_map/dot_general | solution.py:88
  21.7 1.5 fusion.48
  23.2 1.5 fusion.45
  24.7 6.5 %collective-permute-done.1 = bf16[2,192,1024]{2,1,0:T(8,128)(2,1)S(1)} collective-permute-done((bf16[2,192,1024]{2,1,0:T(8,128)(2,1)S(1)}, bf16[2,192,1024]{2,1,0:T(8,128)(2,1)S(1)}, u32[]{:S(2)}, u32[]{:S(2)}) %collective-permute-start.1) | collective-permute-done | bytes 786464 | tf_op jit(solution)/shard_map/ppermute | solution.py:45
  31.3 1.1 convolution_convert_fusion.4
  32.4 1.1 convolution_convert_fusion.5
  33.4 1.1 convolution_convert_fusion.6
  34.6 1.1 convolution_convert_fusion.7
  37.7 1.1 collective-permute-done.9
  38.9 1.4 collective-permute-done.2
  42.7 1.7 %collective-permute-start.10 = (bf16[2,2,4,24,640]{4,3,2,1,0:T(8,128)(2,1)S(1)}, bf16[2,2,4,24,640]{4,3,2,1,0:T(8,128)(2,1)S(1)}, u32[]{:S(2)}, u32[]{:S(2)}) collective-permute-start(bf16[2,2,4,24,640]{4,3,2,1,0:T(8,128)(2,1)S(1)} %pad_maximum_fusion.9), channel_id=1, source_target_pairs={{0,8},{4,28},{8,0},{12,20},{16,24},{20,12},{24,16},{28,4},{1,9},{5... | collective-permute-start | bytes 1474568 | tf_op jit(solution)/shard_map/ppermute | solution.py:45
  45.4 5.9 %collective-permute-done.3 = bf16[2,2,4,24,640]{4,3,2,1,0:T(8,128)(2,1)} collective-permute-done((bf16[2,2,4,24,640]{4,3,2,1,0:T(8,128)(2,1)}, bf16[2,2,4,24,640]{4,3,2,1,0:T(8,128)(2,1)}, u32[]{:S(2)}, u32[]{:S(2)}) %collective-permute-start.3) | collective-permute-done | bytes 491552 | tf_op jit(solution)/shard_map/ppermute | solution.py:45
  51.3 1.0 fusion.120
  52.5 3.7 %collective-permute-start.18 = (bf16[2,192,640]{2,1,0:T(8,128)(2,1)S(1)}, bf16[2,192,640]{2,1,0:T(8,128)(2,1)S(1)}, u32[]{:S(2)}, u32[]{:S(2)}) collective-permute-start(bf16[2,192,640]{2,1,0:T(8,128)(2,1)S(1)} %pad_maximum_fusion.12), channel_id=1, source_target_pairs={{0,3},{1,2},{2,1},{3,0},{4,5},{5,4},{6,7},{7,6},{8,11},{9,10},{10,... | collective-permute-start | bytes 1474568 | tf_op jit(solution)/shard_map/ppermute | solution.py:45
  56.2 1.6 collective-permute-done.10
  57.9 1.9 %collective-permute-start.11 = (bf16[2,4,24,640]{3,2,1,0:T(8,128)(2,1)S(1)}, bf16[2,4,24,640]{3,2,1,0:T(8,128)(2,1)S(1)}, u32[]{:S(2)}, u32[]{:S(2)}) collective-permute-start(bf16[2,4,24,640]{3,2,1,0:T(8,128)(2,1)S(1)} %fusion.117), channel_id=1, source_target_pairs={{0,24},{4,12},{8,16},{12,4},{16,8},{20,28},{24,0},{28,20},{1,25},{... | collective-permute-start | bytes 737288 | tf_op jit(solution)/shard_map/ppermute | solution.py:45
  59.8 1.1 fusion.122
  61.0 1.6 collective-permute-start.5
  62.5 3.0 %collective-permute-done.11 = bf16[2,4,24,640]{3,2,1,0:T(8,128)(2,1)S(1)} collective-permute-done((bf16[2,4,24,640]{3,2,1,0:T(8,128)(2,1)S(1)}, bf16[2,4,24,640]{3,2,1,0:T(8,128)(2,1)S(1)}, u32[]{:S(2)}, u32[]{:S(2)}) %collective-permute-start.11) | collective-permute-done | bytes 245792 | tf_op jit(solution)/shard_map/ppermute | solution.py:45
  65.6 1.6 collective-permute-start.12
  67.4 1.7 %collective-permute-start.6 = (bf16[2,4,24,640]{3,2,1,0:T(8,128)(2,1)S(1)}, bf16[2,4,24,640]{3,2,1,0:T(8,128)(2,1)S(1)}, u32[]{:S(2)}, u32[]{:S(2)}) collective-permute-start(bf16[2,4,24,640]{3,2,1,0:T(8,128)(2,1)S(1)} %fusion.100), channel_id=1, source_target_pairs={{0,24},{4,12},{8,16},{12,4},{16,8},{20,28},{24,0},{28,20},{1,25},{... | collective-permute-start | bytes 737288 | tf_op jit(solution)/shard_map/ppermute | solution.py:45
  69.1 3.4 %collective-permute-done.12 = bf16[2,4,24,640]{3,2,1,0:T(8,128)(2,1)S(1)} collective-permute-done((bf16[2,4,24,640]{3,2,1,0:T(8,128)(2,1)S(1)}, bf16[2,4,24,640]{3,2,1,0:T(8,128)(2,1)S(1)}, u32[]{:S(2)}, u32[]{:S(2)}) %collective-permute-start.12) | collective-permute-done | bytes 245792 | tf_op jit(solution)/shard_map/ppermute | solution.py:45
  72.5 2.6 %collective-permute-start.13 = (bf16[2,4,24,640]{3,2,1,0:T(8,128)(2,1)S(1)}, bf16[2,4,24,640]{3,2,1,0:T(8,128)(2,1)S(1)}, u32[]{:S(2)}, u32[]{:S(2)}) collective-permute-start(bf16[2,4,24,640]{3,2,1,0:T(8,128)(2,1)S(1)} %add_convert_fusion.3), channel_id=1, source_target_pairs={{0,96},{32,64},{64,32},{96,0},{4,36},{36,4},{68,100},{100,68},{8,1... | collective-permute-start | bytes 737288 | tf_op jit(solution)/shard_map/ppermute | solution.py:45
  75.5 4.5 %collective-permute-done.13 = bf16[2,4,24,640]{3,2,1,0:T(8,128)(2,1)S(1)} collective-permute-done((bf16[2,4,24,640]{3,2,1,0:T(8,128)(2,1)S(1)}, bf16[2,4,24,640]{3,2,1,0:T(8,128)(2,1)S(1)}, u32[]{:S(2)}, u32[]{:S(2)}) %collective-permute-start.13) | collective-permute-done | bytes 245792 | tf_op jit(solution)/shard_map/ppermute | solution.py:45
  80.3 2.8 %collective-permute-start.14 = (bf16[2,4,24,640]{3,2,1,0:T(8,128)(2,1)S(1)}, bf16[2,4,24,640]{3,2,1,0:T(8,128)(2,1)S(1)}, u32[]{:S(2)}, u32[]{:S(2)}) collective-permute-start(bf16[2,4,24,640]{3,2,1,0:T(8,128)(2,1)S(1)} %get-tuple-element.3), channel_id=1, source_target_pairs={{0,24},{4,12},{8,16},{12,4},{16,8},{20,28},{24,0},{28,20},{1,25},{... | collective-permute-start | bytes 737288 | tf_op jit(solution)/shard_map/ppermute | solution.py:45
  83.3 7.1 %collective-permute-done.14 = bf16[2,4,24,640]{3,2,1,0:T(8,128)(2,1)S(1)} collective-permute-done((bf16[2,4,24,640]{3,2,1,0:T(8,128)(2,1)S(1)}, bf16[2,4,24,640]{3,2,1,0:T(8,128)(2,1)S(1)}, u32[]{:S(2)}, u32[]{:S(2)}) %collective-permute-start.14) | collective-permute-done | bytes 245792 | tf_op jit(solution)/shard_map/ppermute | solution.py:45
  90.6 1.5 collective-permute-done.7
  94.0 5.4 %collective-permute-done.15 = bf16[2,2,4,24,640]{4,3,2,1,0:T(8,128)(2,1)S(1)} collective-permute-done((bf16[2,2,4,24,640]{4,3,2,1,0:T(8,128)(2,1)S(1)}, bf16[2,2,4,24,640]{4,3,2,1,0:T(8,128)(2,1)S(1)}, u32[]{:S(2)}, u32[]{:S(2)}) %collective-permute-start.15) | collective-permute-done | bytes 491552 | tf_op jit(solution)/shard_map/ppermute | solution.py:45
  103.2 7.9 %collective-permute-done.19 = bf16[2,96,1024]{2,1,0:T(8,128)(2,1)S(1)} collective-permute-done((bf16[2,96,1024]{2,1,0:T(8,128)(2,1)S(1)}, bf16[2,96,1024]{2,1,0:T(8,128)(2,1)S(1)}, u32[]{:S(2)}, u32[]{:S(2)}) %collective-permute-start.19) | collective-permute-done | bytes 393248 | tf_op jit(solution)/shard_map/ppermute | solution.py:45
  111.2 3.7 %collective-permute-start.20 = (bf16[96,1024]{1,0:T(8,128)(2,1)S(1)}, bf16[96,1024]{1,0:T(8,128)(2,1)S(1)}, u32[]{:S(2)}, u32[]{:S(2)}) collective-permute-start(bf16[96,1024]{1,0:T(8,128)(2,1)S(1)} %fusion.154), channel_id=1, source_target_pairs={{0,3},{1,2},{2,1},{3,0},{4,5},{5,4},{6,7},{7,6},{8,11},{9,10},{10,... | collective-permute-start | bytes 589832 | tf_op jit(solution)/shard_map/ppermute | solution.py:45
  117.7 2.5 %fusion.9 = bf16[1,1024,640]{2,1,0:T(8,128)(2,1)S(1)} fusion(bf16[768,640]{1,0:T(8,128)(2,1)S(1)} %bitcast.374, bf16[192,1024]{1,0:T(8,128)(2,1)S(1)} %copy-done.7, bf16[192,1024]{1,0:T(8,128)(2,1)S(1)} %copy-done.3, bf16[192,1024]{1,0:T(8,128)(2,1)S(1)} %copy-done.5, bf16[192,1024]{1,0:T(8,128)(2,1)} %get-tuple-element.71), kind=kOutput, calls=%fused_computation.28 | convolution fusion | flops 1013579776 | bytes 3866624 | tf_op jit(solution)/shard_map/dot_general | solution.py:155
  120.2 2.4 %fusion.10 = bf16[1,1024,640]{2,1,0:T(8,128)(2,1)S(1)} fusion(bf16[768,640]{1,0:T(8,128)(2,1)S(1)} %bitcast.375, bf16[192,1024]{1,0:T(8,128)(2,1)S(1)} %copy-done.7, bf16[192,1024]{1,0:T(8,128)(2,1)S(1)} %copy-done.3, bf16[192,1024]{1,0:T(8,128)(2,1)S(1)} %copy-done.5, bf16[192,1024]{1,0:T(8,128)(2,1)} %get-tuple-element.71), kind=kOutput, calls=%fused_computation.29 | convolution fusion | flops 1013579776 | bytes 3866624 | tf_op jit(solution)/shard_map/dot_general | solution.py:155
  125.2 8.5 %collective-permute-done.22 = bf16[2,96,1024]{2,1,0:T(8,128)(2,1)S(1)} collective-permute-done((bf16[2,96,1024]{2,1,0:T(8,128)(2,1)S(1)}, bf16[2,96,1024]{2,1,0:T(8,128)(2,1)S(1)}, u32[]{:S(2)}, u32[]{:S(2)}) %collective-permute-start.22) | collective-permute-done | bytes 393248 | tf_op jit(solution)/shard_map/ppermute | solution.py:45
  134.5 2.4 %fusion.11 = bf16[1,1024,640]{2,1,0:T(8,128)(2,1)S(1)} fusion(bf16[768,640]{1,0:T(8,128)(2,1)S(1)} %bitcast.373, bf16[192,1024]{1,0:T(8,128)(2,1)S(1)} %copy-done.7, bf16[192,1024]{1,0:T(8,128)(2,1)S(1)} %copy-done.3, bf16[192,1024]{1,0:T(8,128)(2,1)S(1)} %copy-done.5, bf16[192,1024]{1,0:T(8,128)(2,1)} %get-tuple-element.71), kind=kOutput, calls=%fused_computation.30 | convolution fusion | flops 1013579776 | bytes 3866624 | tf_op jit(solution)/shard_map/dot_general | solution.py:155
  136.9 5.7 %collective-permute-done.23 = bf16[96,1024]{1,0:T(8,128)(2,1)S(1)} collective-permute-done((bf16[96,1024]{1,0:T(8,128)(2,1)S(1)}, bf16[96,1024]{1,0:T(8,128)(2,1)S(1)}, u32[]{:S(2)}, u32[]{:S(2)}) %collective-permute-start.23) | collective-permute-done | bytes 196640 | tf_op jit(solution)/shard_map/ppermute | solution.py:45
  143.2 3.2 %collective-permute-start.24 = (bf16[96,1024]{1,0:T(8,128)(2,1)S(1)}, bf16[96,1024]{1,0:T(8,128)(2,1)S(1)}, u32[]{:S(2)}, u32[]{:S(2)}) collective-permute-start(bf16[96,1024]{1,0:T(8,128)(2,1)S(1)} %get-tuple-element.33), channel_id=1, source_target_pairs={{0,3},{1,2},{2,1},{3,0},{4,5},{5,4},{6,7},{7,6},{8,11},{9,10},{10,... | collective-permute-start | bytes 589832 | tf_op jit(solution)/shard_map/ppermute | solution.py:45
  146.4 2.5 %fusion.12 = bf16[1,1024,640]{2,1,0:T(8,128)(2,1)S(1)} fusion(bf16[768,640]{1,0:T(8,128)(2,1)S(1)} %bitcast.372, bf16[192,1024]{1,0:T(8,128)(2,1)S(1)} %copy-done.7, bf16[192,1024]{1,0:T(8,128)(2,1)S(1)} %copy-done.3, bf16[192,1024]{1,0:T(8,128)(2,1)S(1)} %copy-done.5, bf16[192,1024]{1,0:T(8,128)(2,1)} %get-tuple-element.71), kind=kOutput, calls=%fused_computation.31 | convolution fusion | flops 1013579776 | bytes 3866624 | tf_op jit(solution)/shard_map/dot_general | solution.py:155
  148.9 2.4 %collective-permute-done.21 = bf16[96,1024]{1,0:T(8,128)(2,1)S(1)} collective-permute-done((bf16[96,1024]{1,0:T(8,128)(2,1)S(1)}, bf16[96,1024]{1,0:T(8,128)(2,1)S(1)}, u32[]{:S(2)}, u32[]{:S(2)}) %collective-permute-start.21) | collective-permute-done | bytes 196640 | tf_op jit(solution)/shard_map/ppermute | solution.py:45
  151.4 2.0 %collective-permute-done.24 = bf16[96,1024]{1,0:T(8,128)(2,1)S(1)} collective-permute-done((bf16[96,1024]{1,0:T(8,128)(2,1)S(1)}, bf16[96,1024]{1,0:T(8,128)(2,1)S(1)}, u32[]{:S(2)}, u32[]{:S(2)}) %collective-permute-start.24) | collective-permute-done | bytes 196640 | tf_op jit(solution)/shard_map/ppermute | solution.py:45
  153.6 2.9 %maximum_bitcast_fusion = bf16[1,4,1024,640]{3,2,1,0:T(8,128)(2,1)} fusion(bf16[1,1024,640]{2,1,0:T(8,128)(2,1)S(1)} %fusion.12, bf16[1,1024,640]{2,1,0:T(8,128)(2,1)S(1)} %fusion.11, bf16[1,1024,640]{2,1,0:T(8,128)(2,1)S(1)} %fusion.10, bf16[1,1024,640]{2,1,0:T(8,128)(2,1)S(1)} %fusion.9), kind=kLoop, calls=%fused_computation | loop fusion | flops 7864320 | bytes 10485760 | tf_op jit(solution)/shard_map/broadcast_in_dim | solution.py:192
  156.5 2.7 %collective-permute-done.25 = bf16[2,96,1024]{2,1,0:T(8,128)(2,1)S(1)} collective-permute-done((bf16[2,96,1024]{2,1,0:T(8,128)(2,1)S(1)}, bf16[2,96,1024]{2,1,0:T(8,128)(2,1)S(1)}, u32[]{:S(2)}, u32[]{:S(2)}) %collective-permute-start.25) | collective-permute-done | bytes 393248 | tf_op jit(solution)/shard_map/ppermute | solution.py:45
  159.2 4.2 %collective-permute-done.26 = bf16[2,96,1024]{2,1,0:T(8,128)(2,1)S(1)} collective-permute-done((bf16[2,96,1024]{2,1,0:T(8,128)(2,1)S(1)}, bf16[2,96,1024]{2,1,0:T(8,128)(2,1)S(1)}, u32[]{:S(2)}, u32[]{:S(2)}) %collective-permute-start.26) | collective-permute-done | bytes 393248 | tf_op jit(solution)/shard_map/ppermute | solution.py:45
  164.3 2.0 %fusion.8 = bf16[1,640,1024]{2,1,0:T(8,128)(2,1)} fusion(f32[640,1024]{1,0:T(8,128)S(1)} %fusion.89, bf16[96,1024]{1,0:T(8,128)(2,1)S(1)} %collective-permute-done.24, bf16[96,1024]{1,0:T(8,128)(2,1)S(1)} %get-tuple-element.33, bf16[96,1024]{1,0:T(8,128)(2,1)S(1)} %collective-permute-done.21, bf16[96,1024]{1,0:T(8,128)(2,1)S(1)} %get-tuple-element.32, ...), kind=kOutput, calls=%fused_computation.27 | convolution fusion | flops 509739008 | bytes 5210112 | tf_op jit(solution)/shard_map/dot_general | solution.py:155
  (134 shorter events, 22.3 us)
Async XLA Ops:
  0.6 7.9 %copy-start.1 = (bf16[1,192,2560]{2,1,0:T(8,128)(2,1)S(1)}, bf16[1,192,2560]{2,1,0:T(8,128)(2,1)}, u32[]{:S(2)}) copy-start(bf16[1,192,2560]{2,1,0:T(8,128)(2,1)} %param.10) | copy-start | bytes 2949124
  5.5 12.5 %collective-permute-start = (bf16[192,1024]{1,0:T(8,128)(2,1)}, bf16[192,1024]{1,0:T(8,128)(2,1)S(1)}, u32[]{:S(2)}, u32[]{:S(2)}) collective-permute-start(bf16[192,1024]{1,0:T(8,128)(2,1)} %get-tuple-element.71), channel_id=1, source_target_pairs={{0,3},{1,2},{2,1},{3,0},{4,5},{5,4},{6,7},{7,6},{8,11},{9,10},{10,... | collective-permute-start | bytes 1179656 | tf_op jit(solution)/shard_map/ppermute | solution.py:45
  8.6 1.1 copy-start.9
  9.6 34.9 %collective-permute-start.17 = (bf16[2,192,640]{2,1,0:T(8,128)(2,1)}, bf16[2,192,640]{2,1,0:T(8,128)(2,1)}, u32[]{:S(2)}, u32[]{:S(2)}) collective-permute-start(bf16[2,192,640]{2,1,0:T(8,128)(2,1)} %pad_maximum_fusion.11), channel_id=1, source_target_pairs={{0,1},{1,0},{2,3},{3,2},{4,7},{5,6},{6,5},{7,4},{8,9},{9,8},{10,11... | collective-permute-start | bytes 1474568 | tf_op jit(solution)/shard_map/ppermute | solution.py:45
  9.7 11.9 %copy-start = (bf16[1,4,1024,640]{3,2,1,0:T(8,128)(2,1)S(1)}, bf16[1,4,1024,640]{3,2,1,0:T(8,128)(2,1)}, u32[]{:S(2)}) copy-start(bf16[1,4,1024,640]{3,2,1,0:T(8,128)(2,1)} %param.13) | copy-start | bytes 15728644
  19.1 12.1 %collective-permute-start.1 = (bf16[2,192,1024]{2,1,0:T(8,128)(2,1)S(1)}, bf16[2,192,1024]{2,1,0:T(8,128)(2,1)S(1)}, u32[]{:S(2)}, u32[]{:S(2)}) collective-permute-start(bf16[2,192,1024]{2,1,0:T(8,128)(2,1)S(1)} %pad_maximum_fusion.6), channel_id=1, source_target_pairs={{0,1},{1,0},{2,3},{3,2},{4,7},{5,6},{6,5},{7,4},{8,9},{9,8},{10,11... | collective-permute-start | bytes 2359304 | tf_op jit(solution)/shard_map/ppermute | solution.py:45
  31.2 3.4 %copy-start.2 = (bf16[192,1024]{1,0:T(8,128)(2,1)}, bf16[192,1024]{1,0:T(8,128)(2,1)S(1)}, u32[]{:S(2)}) copy-start(bf16[192,1024]{1,0:T(8,128)(2,1)S(1)} %slice_bitcast_fusion) | copy-start | bytes 1179652
  31.2 3.3 %copy-start.4 = (bf16[192,1024]{1,0:T(8,128)(2,1)}, bf16[192,1024]{1,0:T(8,128)(2,1)S(1)}, u32[]{:S(2)}) copy-start(bf16[192,1024]{1,0:T(8,128)(2,1)S(1)} %get-tuple-element.4) | copy-start | bytes 1179652
  31.2 3.3 %copy-start.6 = (bf16[192,1024]{1,0:T(8,128)(2,1)}, bf16[192,1024]{1,0:T(8,128)(2,1)S(1)}, u32[]{:S(2)}) copy-start(bf16[192,1024]{1,0:T(8,128)(2,1)S(1)} %get-tuple-element.5) | copy-start | bytes 1179652
  36.2 2.6 %collective-permute-start.9 = (bf16[2,4,96,640]{3,2,1,0:T(8,128)(2,1)S(1)}, bf16[2,4,96,640]{3,2,1,0:T(8,128)(2,1)S(1)}, u32[]{:S(2)}, u32[]{:S(2)}) collective-permute-start(bf16[2,4,96,640]{3,2,1,0:T(8,128)(2,1)S(1)} %fusion.58), channel_id=1, source_target_pairs={{0,4},{4,0},{8,12},{12,8},{16,20},{20,16},{24,28},{28,24},{1,5},{5... | collective-permute-start | bytes 2949128 | tf_op jit(solution)/shard_map/ppermute | solution.py:28
  36.8 0.7 copy-start.10
  36.8 0.9 copy-start.8
  37.0 3.4 %collective-permute-start.2 = (bf16[2,4,96,640]{3,2,1,0:T(8,128)(2,1)S(1)}, bf16[2,4,96,640]{3,2,1,0:T(8,128)(2,1)S(1)}, u32[]{:S(2)}, u32[]{:S(2)}) collective-permute-start(bf16[2,4,96,640]{3,2,1,0:T(8,128)(2,1)S(1)} %fusion.62), channel_id=1, source_target_pairs={{0,4},{4,0},{8,12},{12,8},{16,20},{20,16},{24,28},{28,24},{1,5},{5... | collective-permute-start | bytes 2949128 | tf_op jit(solution)/shard_map/ppermute | solution.py:28
  42.2 9.1 %collective-permute-start.3 = (bf16[2,2,4,24,640]{4,3,2,1,0:T(8,128)(2,1)}, bf16[2,2,4,24,640]{4,3,2,1,0:T(8,128)(2,1)}, u32[]{:S(2)}, u32[]{:S(2)}) collective-permute-start(bf16[2,2,4,24,640]{4,3,2,1,0:T(8,128)(2,1)} %pad_maximum_fusion.7), channel_id=1, source_target_pairs={{0,8},{4,28},{8,0},{12,20},{16,24},{20,12},{24,16},{28,4},{1,9},{5... | collective-permute-start | bytes 1474568 | tf_op jit(solution)/shard_map/ppermute | solution.py:45
  42.7 15.0 %collective-permute-start.10 = (bf16[2,2,4,24,640]{4,3,2,1,0:T(8,128)(2,1)S(1)}, bf16[2,2,4,24,640]{4,3,2,1,0:T(8,128)(2,1)S(1)}, u32[]{:S(2)}, u32[]{:S(2)}) collective-permute-start(bf16[2,2,4,24,640]{4,3,2,1,0:T(8,128)(2,1)S(1)} %pad_maximum_fusion.9), channel_id=1, source_target_pairs={{0,8},{4,28},{8,0},{12,20},{16,24},{20,12},{24,16},{28,4},{1,9},{5... | collective-permute-start | bytes 1474568 | tf_op jit(solution)/shard_map/ppermute | solution.py:45
  52.4 7.5 %collective-permute-start.4 = (bf16[2,4,24,640]{3,2,1,0:T(8,128)(2,1)S(1)}, bf16[2,4,24,640]{3,2,1,0:T(8,128)(2,1)S(1)}, u32[]{:S(2)}, u32[]{:S(2)}) collective-permute-start(bf16[2,4,24,640]{3,2,1,0:T(8,128)(2,1)S(1)} %fusion.120), channel_id=1, source_target_pairs={{0,24},{4,12},{8,16},{12,4},{16,8},{20,28},{24,0},{28,20},{1,25},{... | collective-permute-start | bytes 737288 | tf_op jit(solution)/shard_map/ppermute | solution.py:45
  52.5 50.6 %collective-permute-start.18 = (bf16[2,192,640]{2,1,0:T(8,128)(2,1)S(1)}, bf16[2,192,640]{2,1,0:T(8,128)(2,1)S(1)}, u32[]{:S(2)}, u32[]{:S(2)}) collective-permute-start(bf16[2,192,640]{2,1,0:T(8,128)(2,1)S(1)} %pad_maximum_fusion.12), channel_id=1, source_target_pairs={{0,3},{1,2},{2,1},{3,0},{4,5},{5,4},{6,7},{7,6},{8,11},{9,10},{10,... | collective-permute-start | bytes 1474568 | tf_op jit(solution)/shard_map/ppermute | solution.py:45
  57.9 7.7 %collective-permute-start.11 = (bf16[2,4,24,640]{3,2,1,0:T(8,128)(2,1)S(1)}, bf16[2,4,24,640]{3,2,1,0:T(8,128)(2,1)S(1)}, u32[]{:S(2)}, u32[]{:S(2)}) collective-permute-start(bf16[2,4,24,640]{3,2,1,0:T(8,128)(2,1)S(1)} %fusion.117), channel_id=1, source_target_pairs={{0,24},{4,12},{8,16},{12,4},{16,8},{20,28},{24,0},{28,20},{1,25},{... | collective-permute-start | bytes 737288 | tf_op jit(solution)/shard_map/ppermute | solution.py:45
  60.9 31.4 %slice-start = ((s8[5242880]{0:T(1024)(128)(4,1)}), s8[4194304]{0:T(1024)(128)(4,1)S(1)}, s32[]{:S(2)}) async-start(s8[5242880]{0:T(1024)(128)(4,1)} %bitcast.349), calls=%async_computation | async-start | bytes 8388608
  61.0 6.2 %collective-permute-start.5 = (bf16[1,4,24,640]{3,2,1,0:T(8,128)(2,1)S(1)}, bf16[1,4,24,640]{3,2,1,0:T(8,128)(2,1)S(1)}, u32[]{:S(2)}, u32[]{:S(2)}) collective-permute-start(bf16[1,4,24,640]{3,2,1,0:T(8,128)(2,1)S(1)} %get-tuple-element.63), channel_id=1, source_target_pairs={{0,32},{32,0},{64,96},{96,64},{4,36},{36,4},{68,100},{100,68},{8,4... | collective-permute-start | bytes 368648 | tf_op jit(solution)/shard_map/ppermute | solution.py:45
  65.6 6.8 %collective-permute-start.12 = (bf16[2,4,24,640]{3,2,1,0:T(8,128)(2,1)S(1)}, bf16[2,4,24,640]{3,2,1,0:T(8,128)(2,1)S(1)}, u32[]{:S(2)}, u32[]{:S(2)}) collective-permute-start(bf16[2,4,24,640]{3,2,1,0:T(8,128)(2,1)S(1)} %fusion.119), channel_id=1, source_target_pairs={{0,32},{32,0},{64,96},{96,64},{4,100},{36,68},{68,36},{100,4},{8,4... | collective-permute-start | bytes 737288 | tf_op jit(solution)/shard_map/ppermute | solution.py:45
  67.4 15.7 %collective-permute-start.6 = (bf16[2,4,24,640]{3,2,1,0:T(8,128)(2,1)S(1)}, bf16[2,4,24,640]{3,2,1,0:T(8,128)(2,1)S(1)}, u32[]{:S(2)}, u32[]{:S(2)}) collective-permute-start(bf16[2,4,24,640]{3,2,1,0:T(8,128)(2,1)S(1)} %fusion.100), channel_id=1, source_target_pairs={{0,24},{4,12},{8,16},{12,4},{16,8},{20,28},{24,0},{28,20},{1,25},{... | collective-permute-start | bytes 737288 | tf_op jit(solution)/shard_map/ppermute | solution.py:45
  72.5 7.5 %collective-permute-start.13 = (bf16[2,4,24,640]{3,2,1,0:T(8,128)(2,1)S(1)}, bf16[2,4,24,640]{3,2,1,0:T(8,128)(2,1)S(1)}, u32[]{:S(2)}, u32[]{:S(2)}) collective-permute-start(bf16[2,4,24,640]{3,2,1,0:T(8,128)(2,1)S(1)} %add_convert_fusion.3), channel_id=1, source_target_pairs={{0,96},{32,64},{64,32},{96,0},{4,36},{36,4},{68,100},{100,68},{8,1... | collective-permute-start | bytes 737288 | tf_op jit(solution)/shard_map/ppermute | solution.py:45
  75.5 16.8 %slice-start.1 = ((s8[5242880]{0:T(1024)(128)(4,1)}), s8[1048576]{0:T(1024)(128)(4,1)S(1)}, s32[]{:S(2)}) async-start(s8[5242880]{0:T(1024)(128)(4,1)} %bitcast.349), calls=%async_computation.1 | async-start | bytes 2097152
  80.3 10.1 %collective-permute-start.14 = (bf16[2,4,24,640]{3,2,1,0:T(8,128)(2,1)S(1)}, bf16[2,4,24,640]{3,2,1,0:T(8,128)(2,1)S(1)}, u32[]{:S(2)}, u32[]{:S(2)}) collective-permute-start(bf16[2,4,24,640]{3,2,1,0:T(8,128)(2,1)S(1)} %get-tuple-element.3), channel_id=1, source_target_pairs={{0,24},{4,12},{8,16},{12,4},{16,8},{20,28},{24,0},{28,20},{1,25},{... | collective-permute-start | bytes 737288 | tf_op jit(solution)/shard_map/ppermute | solution.py:45
  83.1 8.9 %collective-permute-start.7 = (bf16[2,2,4,24,640]{4,3,2,1,0:T(8,128)(2,1)S(1)}, bf16[2,2,4,24,640]{4,3,2,1,0:T(8,128)(2,1)S(1)}, u32[]{:S(2)}, u32[]{:S(2)}) collective-permute-start(bf16[2,2,4,24,640]{4,3,2,1,0:T(8,128)(2,1)S(1)} %pad_maximum_fusion.8), channel_id=1, source_target_pairs={{0,8},{4,28},{8,0},{12,20},{16,24},{20,12},{24,16},{28,4},{1,9},{5... | collective-permute-start | bytes 1474568 | tf_op jit(solution)/shard_map/ppermute | solution.py:45
  90.4 8.9 %collective-permute-start.15 = (bf16[2,2,4,24,640]{4,3,2,1,0:T(8,128)(2,1)S(1)}, bf16[2,2,4,24,640]{4,3,2,1,0:T(8,128)(2,1)S(1)}, u32[]{:S(2)}, u32[]{:S(2)}) collective-permute-start(bf16[2,2,4,24,640]{4,3,2,1,0:T(8,128)(2,1)S(1)} %pad_maximum_fusion.10), channel_id=1, source_target_pairs={{0,8},{4,28},{8,0},{12,20},{16,24},{20,12},{24,16},{28,4},{1,9},{5... | collective-permute-start | bytes 1474568 | tf_op jit(solution)/shard_map/ppermute | solution.py:45
  92.2 22.7 %collective-permute-start.8 = (bf16[2,384,640]{2,1,0:T(8,128)(2,1)S(1)}, bf16[2,384,640]{2,1,0:T(8,128)(2,1)S(1)}, u32[]{:S(2)}, u32[]{:S(2)}) collective-permute-start(bf16[2,384,640]{2,1,0:T(8,128)(2,1)S(1)} %bitcast.362), channel_id=1, source_target_pairs={{0,4},{4,0},{8,12},{12,8},{16,20},{20,16},{24,28},{28,24},{1,5},{5... | collective-permute-start | bytes 2949128 | tf_op jit(solution)/shard_map/ppermute | solution.py:28
  101.2 10.0 %collective-permute-start.19 = (bf16[2,96,1024]{2,1,0:T(8,128)(2,1)S(1)}, bf16[2,96,1024]{2,1,0:T(8,128)(2,1)S(1)}, u32[]{:S(2)}, u32[]{:S(2)}) collective-permute-start(bf16[2,96,1024]{2,1,0:T(8,128)(2,1)S(1)} %constant_dynamic-slice_fusion.1), channel_id=1, source_target_pairs={{0,1},{1,0},{2,3},{3,2},{4,7},{5,6},{6,5},{7,4},{8,9},{9,8},{10,11... | collective-permute-start | bytes 1179656 | tf_op jit(solution)/shard_map/ppermute | solution.py:45
  103.1 19.5 %collective-permute-start.16 = (bf16[2,384,640]{2,1,0:T(8,128)(2,1)S(1)}, bf16[2,384,640]{2,1,0:T(8,128)(2,1)S(1)}, u32[]{:S(2)}, u32[]{:S(2)}) collective-permute-start(bf16[2,384,640]{2,1,0:T(8,128)(2,1)S(1)} %bitcast.361), channel_id=1, source_target_pairs={{0,4},{4,0},{8,12},{12,8},{16,20},{20,16},{24,28},{28,24},{1,5},{5... | collective-permute-start | bytes 2949128 | tf_op jit(solution)/shard_map/ppermute | solution.py:28
  111.2 25.7 %collective-permute-start.20 = (bf16[96,1024]{1,0:T(8,128)(2,1)S(1)}, bf16[96,1024]{1,0:T(8,128)(2,1)S(1)}, u32[]{:S(2)}, u32[]{:S(2)}) collective-permute-start(bf16[96,1024]{1,0:T(8,128)(2,1)S(1)} %fusion.154), channel_id=1, source_target_pairs={{0,3},{1,2},{2,1},{3,0},{4,5},{5,4},{6,7},{7,6},{8,11},{9,10},{10,... | collective-permute-start | bytes 589832 | tf_op jit(solution)/shard_map/ppermute | solution.py:45
  116.5 1.0 copy-start.3
  116.5 1.1 copy-start.5
  116.5 1.2 copy-start.7
  124.3 9.4 %collective-permute-start.22 = (bf16[2,96,1024]{2,1,0:T(8,128)(2,1)S(1)}, bf16[2,96,1024]{2,1,0:T(8,128)(2,1)S(1)}, u32[]{:S(2)}, u32[]{:S(2)}) collective-permute-start(bf16[2,96,1024]{2,1,0:T(8,128)(2,1)S(1)} %constant_dynamic-slice_fusion), channel_id=1, source_target_pairs={{0,1},{1,0},{2,3},{3,2},{4,7},{5,6},{6,5},{7,4},{8,9},{9,8},{10,11... | collective-permute-start | bytes 1179656 | tf_op jit(solution)/shard_map/ppermute | solution.py:45
  133.8 8.8 %collective-permute-start.23 = (bf16[96,1024]{1,0:T(8,128)(2,1)S(1)}, bf16[96,1024]{1,0:T(8,128)(2,1)S(1)}, u32[]{:S(2)}, u32[]{:S(2)}) collective-permute-start(bf16[96,1024]{1,0:T(8,128)(2,1)S(1)} %fusion.155), channel_id=1, source_target_pairs={{0,3},{1,2},{2,1},{3,0},{4,5},{5,4},{6,7},{7,6},{8,11},{9,10},{10,... | collective-permute-start | bytes 589832 | tf_op jit(solution)/shard_map/ppermute | solution.py:45
  143.1 8.2 %collective-permute-start.21 = (bf16[96,1024]{1,0:T(8,128)(2,1)S(1)}, bf16[96,1024]{1,0:T(8,128)(2,1)S(1)}, u32[]{:S(2)}, u32[]{:S(2)}) collective-permute-start(bf16[96,1024]{1,0:T(8,128)(2,1)S(1)} %get-tuple-element.32), channel_id=1, source_target_pairs={{0,3},{1,2},{2,1},{3,0},{4,5},{5,4},{6,7},{7,6},{8,11},{9,10},{10,... | collective-permute-start | bytes 589832 | tf_op jit(solution)/shard_map/ppermute | solution.py:45
  143.2 10.2 %collective-permute-start.24 = (bf16[96,1024]{1,0:T(8,128)(2,1)S(1)}, bf16[96,1024]{1,0:T(8,128)(2,1)S(1)}, u32[]{:S(2)}, u32[]{:S(2)}) collective-permute-start(bf16[96,1024]{1,0:T(8,128)(2,1)S(1)} %get-tuple-element.33), channel_id=1, source_target_pairs={{0,3},{1,2},{2,1},{3,0},{4,5},{5,4},{6,7},{7,6},{8,11},{9,10},{10,... | collective-permute-start | bytes 589832 | tf_op jit(solution)/shard_map/ppermute | solution.py:45
  151.4 7.9 %collective-permute-start.25 = (bf16[2,96,1024]{2,1,0:T(8,128)(2,1)S(1)}, bf16[2,96,1024]{2,1,0:T(8,128)(2,1)S(1)}, u32[]{:S(2)}, u32[]{:S(2)}) collective-permute-start(bf16[2,96,1024]{2,1,0:T(8,128)(2,1)S(1)} %pad_maximum_fusion.13), channel_id=1, source_target_pairs={{0,1},{1,0},{2,3},{3,2},{4,7},{5,6},{6,5},{7,4},{8,9},{9,8},{10,11... | collective-permute-start | bytes 1179656 | tf_op jit(solution)/shard_map/ppermute | solution.py:45
  153.5 10.0 %collective-permute-start.26 = (bf16[2,96,1024]{2,1,0:T(8,128)(2,1)S(1)}, bf16[2,96,1024]{2,1,0:T(8,128)(2,1)S(1)}, u32[]{:S(2)}, u32[]{:S(2)}) collective-permute-start(bf16[2,96,1024]{2,1,0:T(8,128)(2,1)S(1)} %pad_maximum_fusion.14), channel_id=1, source_target_pairs={{0,1},{1,0},{2,3},{3,2},{4,7},{5,6},{6,5},{7,4},{8,9},{9,8},{10,11... | collective-permute-start | bytes 1179656 | tf_op jit(solution)/shard_map/ppermute | solution.py:45

commit v2 on v1

--- a/solution.py
+++ b/solution.py
@@ -156,6 +156,10 @@
 
     order_m = [m for ms in CHAINS[::-1] for m in ms]
     early, late = [], []
+    far_cols = [
+        jnp.concatenate([cols[2][h * half : (h + 1) * half], cols[3][h * half : (h + 1) * half]], axis=0)
+        for h in range(2)
+    ]
     for h in range(2):
         d_lat = None
         for m in order_m:
@@ -176,11 +180,10 @@
         far = exchange(jnp.stack([d_pre, near]), "token", SIDE_A)
         span = slice(h * half, (h + 1) * half)
         early += [(cols[0][span], d_pre), (cols[1][span], near)]
-        late += [(cols[2][span], far[0]), (cols[3][span], far[1])]
-    enc_total = None
-    for terms in (early, late):
-        prod = outer(*(jnp.concatenate(side, axis=0) for side in zip(*terms)))
-        enc_total = prod if enc_total is None else enc_total + prod
+        late.append((far_cols[h], far.reshape(2 * half, -1)))
+    enc_total = outer(*(jnp.concatenate(side, axis=0) for side in zip(*early)))
+    for h in range(2):
+        enc_total = enc_total + outer(*late[h])
     grad_enc = enc_total.astype(BF16)
 
     lat_all = jnp.concatenate([lat[k] for k in ks], axis=0)

time: 167 us -> 166 us (level)
  waiting for transfers between devices: 81.1 us -> 77.8 us
  starting transfers between devices: 31.6 us -> 33.6 us
    ppermute x23, waiting for transfers between devices: 78.6 us -> 75.2 us  [exchange(): return lax.ppermute(value, names, pairs)]
    ppermute x23, starting transfers between devices: 30.8 us -> 32.7 us  [exchange(): return lax.ppermute(value, names, pairs)]
    dot_general x6 -> x7, matrix products: 12.6 us -> 12.8 us  [outer(): lax.dot_general(left, right, (((0,), (0,)), ((), ())), preferred_element_...]
  transfers between devices with their start and end apart: 27 -> 27, of which waited for: 20 -> 19; matrix products, arithmetic and copies ran while one was open for 26% -> 27% of each run, Pallas kernels for 0% -> 0%
where the time goes in v2:
time: 166 us; the launch traced here: 165 us
  waiting for transfers between devices  77.8 us (47%)
  matrix products  35.5 us (21%)
  starting transfers between devices  33.6 us (20%)
  other arithmetic  12.6 us (8%)
  local copies, waits for them, and re-layouts  4.13 us (2%)
    ppermute x23, waiting for transfers between devices, exchange(): return lax.ppermute(value, names, pairs)  75.2 us
    ppermute x23, starting transfers between devices, exchange(): return lax.ppermute(value, names, pairs)  32.7 us
    dot_general x7, matrix products, outer(): lax.dot_general(left, right, (((0,), (0,)), ((), ())), preferred_element_...  12.8 us
    dot_general x8, matrix products, body(): prod = jnp.dot(lhs, weight[m], preferred_element_type=F32).astype(BF16)  11.3 us
    dot_general x8, matrix products, body(): lax.dot_general(errors[m][h], weight[m], (((1,), (1,)), ((), ())), prefer...  6.44 us
    dot_general x1, matrix products, body(): jnp.dot(res, enc_weight[0], preferred_element_type=F32) + enc_bias[0]  4.9 us
  transfers between devices with their start and end apart: 27, of which 19 were waited for; matrix products, arithmetic and copies ran while one was open for 27% of the time, Pallas kernels for 0%

profile of v2, /device:TPU:96, one launch (start us, length us, event | category | flops | bytes accessed | tf_op | source)
XLA Modules:
  0.0 165.0 jit_solution(17827950706860580838)
XLA Ops:
  0.6 4.9 %multiply_convert_fusion = (bf16[192,1024]{1,0:T(8,128)(2,1)}, f32[192,1024]{1,0:T(8,128)S(1)}) fusion(f32[1024]{0:T(1024)} %bitcast.397, bf16[1,2560,1024]{2,1,0:T(8,128)(2,1)} %param.11, bf16[1,192,2560]{2,1,0:T(8,128)(2,1)} %param.10), kind=kOutput, calls=%fused_computation.119 | convolution fusion | flops 1007812608 | bytes 7409664 | tf_op jit(solution)/shard_map/dot_general | solution.py:75
  5.5 3.0 %collective-permute-start = (bf16[192,1024]{1,0:T(8,128)(2,1)}, bf16[192,1024]{1,0:T(8,128)(2,1)S(1)}, u32[]{:S(2)}, u32[]{:S(2)}) collective-permute-start(bf16[192,1024]{1,0:T(8,128)(2,1)} %get-tuple-element.67), channel_id=1, source_target_pairs={{0,3},{1,2},{2,1},{3,0},{4,5},{5,4},{6,7},{7,6},{8,11},{9,10},{10,... | collective-permute-start | bytes 1179656 | tf_op jit(solution)/shard_map/ppermute | solution.py:45
  9.8 2.1 %fusion.54 = bf16[192,640]{1,0:T(8,128)(2,1)S(1)} fusion(bf16[192,1024]{1,0:T(8,128)(2,1)} %get-tuple-element.67, bf16[1,4,1024,640]{3,2,1,0:T(8,128)(2,1)} %param.13), kind=kOutput, calls=%fused_computation.75 | convolution fusion | flops 251781120 | bytes 1949696 | tf_op jit(solution)/shard_map/dot_general | solution.py:88
  11.8 6.2 %collective-permute-done = bf16[192,1024]{1,0:T(8,128)(2,1)S(1)} collective-permute-done((bf16[192,1024]{1,0:T(8,128)(2,1)}, bf16[192,1024]{1,0:T(8,128)(2,1)S(1)}, u32[]{:S(2)}, u32[]{:S(2)}) %collective-permute-start) | collective-permute-done | bytes 393248 | tf_op jit(solution)/shard_map/ppermute | solution.py:45
  18.0 1.1 pad_maximum_fusion.6
  19.7 1.9 %fusion.51 = bf16[192,640]{1,0:T(8,128)(2,1)S(1)} fusion(bf16[192,1024]{1,0:T(8,128)(2,1)} %get-tuple-element.67, bf16[1,4,1024,640]{3,2,1,0:T(8,128)(2,1)} %param.13), kind=kOutput, calls=%fused_computation.74 | convolution fusion | flops 251781120 | bytes 1949696 | tf_op jit(solution)/shard_map/dot_general | solution.py:88
  21.7 1.5 fusion.48
  23.2 1.5 fusion.45
  24.7 6.5 %collective-permute-done.1 = bf16[2,192,1024]{2,1,0:T(8,128)(2,1)S(1)} collective-permute-done((bf16[2,192,1024]{2,1,0:T(8,128)(2,1)S(1)}, bf16[2,192,1024]{2,1,0:T(8,128)(2,1)S(1)}, u32[]{:S(2)}, u32[]{:S(2)}) %collective-permute-start.1) | collective-permute-done | bytes 786464 | tf_op jit(solution)/shard_map/ppermute | solution.py:45
  31.3 1.1 convolution_convert_fusion.4
  32.4 1.1 convolution_convert_fusion.5
  33.5 1.1 convolution_convert_fusion.6
  34.6 1.1 convolution_convert_fusion.7
  37.8 1.1 collective-permute-done.9
  38.9 1.4 collective-permute-done.2
  42.7 1.7 %collective-permute-start.10 = (bf16[2,2,4,24,640]{4,3,2,1,0:T(8,128)(2,1)S(1)}, bf16[2,2,4,24,640]{4,3,2,1,0:T(8,128)(2,1)S(1)}, u32[]{:S(2)}, u32[]{:S(2)}) collective-permute-start(bf16[2,2,4,24,640]{4,3,2,1,0:T(8,128)(2,1)S(1)} %pad_maximum_fusion.9), channel_id=1, source_target_pairs={{0,8},{4,28},{8,0},{12,20},{16,24},{20,12},{24,16},{28,4},{1,9},{5... | collective-permute-start | bytes 1474568 | tf_op jit(solution)/shard_map/ppermute | solution.py:45
  45.5 5.9 %collective-permute-done.3 = bf16[2,2,4,24,640]{4,3,2,1,0:T(8,128)(2,1)} collective-permute-done((bf16[2,2,4,24,640]{4,3,2,1,0:T(8,128)(2,1)}, bf16[2,2,4,24,640]{4,3,2,1,0:T(8,128)(2,1)}, u32[]{:S(2)}, u32[]{:S(2)}) %collective-permute-start.3) | collective-permute-done | bytes 491552 | tf_op jit(solution)/shard_map/ppermute | solution.py:45
  51.4 1.0 fusion.106
  52.5 3.7 %collective-permute-start.18 = (bf16[2,192,640]{2,1,0:T(8,128)(2,1)S(1)}, bf16[2,192,640]{2,1,0:T(8,128)(2,1)S(1)}, u32[]{:S(2)}, u32[]{:S(2)}) collective-permute-start(bf16[2,192,640]{2,1,0:T(8,128)(2,1)S(1)} %pad_maximum_fusion.12), channel_id=1, source_target_pairs={{0,3},{1,2},{2,1},{3,0},{4,5},{5,4},{6,7},{7,6},{8,11},{9,10},{10,... | collective-permute-start | bytes 1474568 | tf_op jit(solution)/shard_map/ppermute | solution.py:45
  56.2 1.6 collective-permute-done.10
  57.9 1.9 %collective-permute-start.11 = (bf16[2,4,24,640]{3,2,1,0:T(8,128)(2,1)S(1)}, bf16[2,4,24,640]{3,2,1,0:T(8,128)(2,1)S(1)}, u32[]{:S(2)}, u32[]{:S(2)}) collective-permute-start(bf16[2,4,24,640]{3,2,1,0:T(8,128)(2,1)S(1)} %fusion.103), channel_id=1, source_target_pairs={{0,24},{4,12},{8,16},{12,4},{16,8},{20,28},{24,0},{28,20},{1,25},{... | collective-permute-start | bytes 737288 | tf_op jit(solution)/shard_map/ppermute | solution.py:45
  59.9 1.1 fusion.108
  61.0 1.6 collective-permute-start.5
  62.6 3.0 %collective-permute-done.11 = bf16[2,4,24,640]{3,2,1,0:T(8,128)(2,1)S(1)} collective-permute-done((bf16[2,4,24,640]{3,2,1,0:T(8,128)(2,1)S(1)}, bf16[2,4,24,640]{3,2,1,0:T(8,128)(2,1)S(1)}, u32[]{:S(2)}, u32[]{:S(2)}) %collective-permute-start.11) | collective-permute-done | bytes 245792 | tf_op jit(solution)/shard_map/ppermute | solution.py:45
  65.7 1.6 collective-permute-start.12
  67.4 1.7 %collective-permute-start.6 = (bf16[2,4,24,640]{3,2,1,0:T(8,128)(2,1)S(1)}, bf16[2,4,24,640]{3,2,1,0:T(8,128)(2,1)S(1)}, u32[]{:S(2)}, u32[]{:S(2)}) collective-permute-start(bf16[2,4,24,640]{3,2,1,0:T(8,128)(2,1)S(1)} %fusion.93), channel_id=1, source_target_pairs={{0,24},{4,12},{8,16},{12,4},{16,8},{20,28},{24,0},{28,20},{1,25},{... | collective-permute-start | bytes 737288 | tf_op jit(solution)/shard_map/ppermute | solution.py:45
  69.1 3.4 %collective-permute-done.12 = bf16[2,4,24,640]{3,2,1,0:T(8,128)(2,1)S(1)} collective-permute-done((bf16[2,4,24,640]{3,2,1,0:T(8,128)(2,1)S(1)}, bf16[2,4,24,640]{3,2,1,0:T(8,128)(2,1)S(1)}, u32[]{:S(2)}, u32[]{:S(2)}) %collective-permute-start.12) | collective-permute-done | bytes 245792 | tf_op jit(solution)/shard_map/ppermute | solution.py:45
  72.6 2.6 %collective-permute-start.13 = (bf16[2,4,24,640]{3,2,1,0:T(8,128)(2,1)S(1)}, bf16[2,4,24,640]{3,2,1,0:T(8,128)(2,1)S(1)}, u32[]{:S(2)}, u32[]{:S(2)}) collective-permute-start(bf16[2,4,24,640]{3,2,1,0:T(8,128)(2,1)S(1)} %add_convert_fusion.3), channel_id=1, source_target_pairs={{0,96},{32,64},{64,32},{96,0},{4,36},{36,4},{68,100},{100,68},{8,1... | collective-permute-start | bytes 737288 | tf_op jit(solution)/shard_map/ppermute | solution.py:45
  75.5 4.6 %collective-permute-done.13 = bf16[2,4,24,640]{3,2,1,0:T(8,128)(2,1)S(1)} collective-permute-done((bf16[2,4,24,640]{3,2,1,0:T(8,128)(2,1)S(1)}, bf16[2,4,24,640]{3,2,1,0:T(8,128)(2,1)S(1)}, u32[]{:S(2)}, u32[]{:S(2)}) %collective-permute-start.13) | collective-permute-done | bytes 245792 | tf_op jit(solution)/shard_map/ppermute | solution.py:45
  80.3 2.8 %collective-permute-start.14 = (bf16[2,4,24,640]{3,2,1,0:T(8,128)(2,1)S(1)}, bf16[2,4,24,640]{3,2,1,0:T(8,128)(2,1)S(1)}, u32[]{:S(2)}, u32[]{:S(2)}) collective-permute-start(bf16[2,4,24,640]{3,2,1,0:T(8,128)(2,1)S(1)} %get-tuple-element.3), channel_id=1, source_target_pairs={{0,24},{4,12},{8,16},{12,4},{16,8},{20,28},{24,0},{28,20},{1,25},{... | collective-permute-start | bytes 737288 | tf_op jit(solution)/shard_map/ppermute | solution.py:45
  83.3 7.1 %collective-permute-done.14 = bf16[2,4,24,640]{3,2,1,0:T(8,128)(2,1)S(1)} collective-permute-done((bf16[2,4,24,640]{3,2,1,0:T(8,128)(2,1)S(1)}, bf16[2,4,24,640]{3,2,1,0:T(8,128)(2,1)S(1)}, u32[]{:S(2)}, u32[]{:S(2)}) %collective-permute-start.14) | collective-permute-done | bytes 245792 | tf_op jit(solution)/shard_map/ppermute | solution.py:45
  90.6 1.4 collective-permute-done.7
  94.0 5.4 %collective-permute-done.15 = bf16[2,2,4,24,640]{4,3,2,1,0:T(8,128)(2,1)S(1)} collective-permute-done((bf16[2,2,4,24,640]{4,3,2,1,0:T(8,128)(2,1)S(1)}, bf16[2,2,4,24,640]{4,3,2,1,0:T(8,128)(2,1)S(1)}, u32[]{:S(2)}, u32[]{:S(2)}) %collective-permute-start.15) | collective-permute-done | bytes 491552 | tf_op jit(solution)/shard_map/ppermute | solution.py:45
  103.3 7.9 %collective-permute-done.19 = bf16[2,96,1024]{2,1,0:T(8,128)(2,1)S(1)} collective-permute-done((bf16[2,96,1024]{2,1,0:T(8,128)(2,1)S(1)}, bf16[2,96,1024]{2,1,0:T(8,128)(2,1)S(1)}, u32[]{:S(2)}, u32[]{:S(2)}) %collective-permute-start.19) | collective-permute-done | bytes 393248 | tf_op jit(solution)/shard_map/ppermute | solution.py:45
  111.2 3.7 %collective-permute-start.20 = (bf16[96,1024]{1,0:T(8,128)(2,1)S(1)}, bf16[96,1024]{1,0:T(8,128)(2,1)S(1)}, u32[]{:S(2)}, u32[]{:S(2)}) collective-permute-start(bf16[96,1024]{1,0:T(8,128)(2,1)S(1)} %fusion.150), channel_id=1, source_target_pairs={{0,3},{1,2},{2,1},{3,0},{4,5},{5,4},{6,7},{7,6},{8,11},{9,10},{10,... | collective-permute-start | bytes 589832 | tf_op jit(solution)/shard_map/ppermute | solution.py:45
  117.7 2.5 %fusion.8 = bf16[1,1024,640]{2,1,0:T(8,128)(2,1)S(1)} fusion(bf16[768,640]{1,0:T(8,128)(2,1)S(1)} %bitcast.370, bf16[192,1024]{1,0:T(8,128)(2,1)S(1)} %copy-done.7, bf16[192,1024]{1,0:T(8,128)(2,1)S(1)} %copy-done.3, bf16[192,1024]{1,0:T(8,128)(2,1)S(1)} %copy-done.5, bf16[192,1024]{1,0:T(8,128)(2,1)} %get-tuple-element.67), kind=kOutput, calls=%fused_computation.27 | convolution fusion | flops 1013579776 | bytes 3866624 | tf_op jit(solution)/shard_map/dot_general | solution.py:155
  120.2 2.4 %fusion.9 = bf16[1,1024,640]{2,1,0:T(8,128)(2,1)S(1)} fusion(bf16[768,640]{1,0:T(8,128)(2,1)S(1)} %bitcast.371, bf16[192,1024]{1,0:T(8,128)(2,1)S(1)} %copy-done.7, bf16[192,1024]{1,0:T(8,128)(2,1)S(1)} %copy-done.3, bf16[192,1024]{1,0:T(8,128)(2,1)S(1)} %copy-done.5, bf16[192,1024]{1,0:T(8,128)(2,1)} %get-tuple-element.67), kind=kOutput, calls=%fused_computation.28 | convolution fusion | flops 1013579776 | bytes 3866624 | tf_op jit(solution)/shard_map/dot_general | solution.py:155
  125.2 8.5 %collective-permute-done.22 = bf16[2,96,1024]{2,1,0:T(8,128)(2,1)S(1)} collective-permute-done((bf16[2,96,1024]{2,1,0:T(8,128)(2,1)S(1)}, bf16[2,96,1024]{2,1,0:T(8,128)(2,1)S(1)}, u32[]{:S(2)}, u32[]{:S(2)}) %collective-permute-start.22) | collective-permute-done | bytes 393248 | tf_op jit(solution)/shard_map/ppermute | solution.py:45
  134.5 2.4 %fusion.10 = bf16[1,1024,640]{2,1,0:T(8,128)(2,1)S(1)} fusion(bf16[768,640]{1,0:T(8,128)(2,1)S(1)} %bitcast.369, bf16[192,1024]{1,0:T(8,128)(2,1)S(1)} %copy-done.7, bf16[192,1024]{1,0:T(8,128)(2,1)S(1)} %copy-done.3, bf16[192,1024]{1,0:T(8,128)(2,1)S(1)} %copy-done.5, bf16[192,1024]{1,0:T(8,128)(2,1)} %get-tuple-element.67), kind=kOutput, calls=%fused_computation.29 | convolution fusion | flops 1013579776 | bytes 3866624 | tf_op jit(solution)/shard_map/dot_general | solution.py:155
  136.9 5.7 %collective-permute-done.23 = bf16[96,1024]{1,0:T(8,128)(2,1)S(1)} collective-permute-done((bf16[96,1024]{1,0:T(8,128)(2,1)S(1)}, bf16[96,1024]{1,0:T(8,128)(2,1)S(1)}, u32[]{:S(2)}, u32[]{:S(2)}) %collective-permute-start.23) | collective-permute-done | bytes 196640 | tf_op jit(solution)/shard_map/ppermute | solution.py:45
  143.2 2.5 %fusion.11 = bf16[1,1024,640]{2,1,0:T(8,128)(2,1)S(1)} fusion(bf16[768,640]{1,0:T(8,128)(2,1)S(1)} %bitcast.368, bf16[192,1024]{1,0:T(8,128)(2,1)S(1)} %copy-done.7, bf16[192,1024]{1,0:T(8,128)(2,1)S(1)} %copy-done.3, bf16[192,1024]{1,0:T(8,128)(2,1)S(1)} %copy-done.5, bf16[192,1024]{1,0:T(8,128)(2,1)} %get-tuple-element.67), kind=kOutput, calls=%fused_computation.30 | convolution fusion | flops 1013579776 | bytes 3866624 | tf_op jit(solution)/shard_map/dot_general | solution.py:155
  145.7 3.3 %collective-permute-start.24 = (bf16[96,1024]{1,0:T(8,128)(2,1)S(1)}, bf16[96,1024]{1,0:T(8,128)(2,1)S(1)}, u32[]{:S(2)}, u32[]{:S(2)}) collective-permute-start(bf16[96,1024]{1,0:T(8,128)(2,1)S(1)} %get-tuple-element.33), channel_id=1, source_target_pairs={{0,3},{1,2},{2,1},{3,0},{4,5},{5,4},{6,7},{7,6},{8,11},{9,10},{10,... | collective-permute-start | bytes 589832 | tf_op jit(solution)/shard_map/ppermute | solution.py:45
  149.0 2.3 %collective-permute-done.21 = bf16[96,1024]{1,0:T(8,128)(2,1)S(1)} collective-permute-done((bf16[96,1024]{1,0:T(8,128)(2,1)S(1)}, bf16[96,1024]{1,0:T(8,128)(2,1)S(1)}, u32[]{:S(2)}, u32[]{:S(2)}) %collective-permute-start.21) | collective-permute-done | bytes 196640 | tf_op jit(solution)/shard_map/ppermute | solution.py:45
  151.5 3.0 %maximum_bitcast_fusion = bf16[1,4,1024,640]{3,2,1,0:T(8,128)(2,1)} fusion(bf16[1,1024,640]{2,1,0:T(8,128)(2,1)S(1)} %fusion.11, bf16[1,1024,640]{2,1,0:T(8,128)(2,1)S(1)} %fusion.10, bf16[1,1024,640]{2,1,0:T(8,128)(2,1)S(1)} %fusion.9, bf16[1,1024,640]{2,1,0:T(8,128)(2,1)S(1)} %fusion.8), kind=kLoop, calls=%fused_computation | loop fusion | flops 7864320 | bytes 10485760 | tf_op jit(solution)/shard_map/broadcast_in_dim | solution.py:195
  154.5 2.1 %collective-permute-start.26 = (bf16[2,96,1024]{2,1,0:T(8,128)(2,1)S(1)}, bf16[2,96,1024]{2,1,0:T(8,128)(2,1)S(1)}, u32[]{:S(2)}, u32[]{:S(2)}) collective-permute-start(bf16[2,96,1024]{2,1,0:T(8,128)(2,1)S(1)} %pad_maximum_fusion.14), channel_id=1, source_target_pairs={{0,1},{1,0},{2,3},{3,2},{4,7},{5,6},{6,5},{7,4},{8,9},{9,8},{10,11... | collective-permute-start | bytes 1179656 | tf_op jit(solution)/shard_map/ppermute | solution.py:45
  157.4 1.8 %collective-permute-done.25 = bf16[2,96,1024]{2,1,0:T(8,128)(2,1)S(1)} collective-permute-done((bf16[2,96,1024]{2,1,0:T(8,128)(2,1)S(1)}, bf16[2,96,1024]{2,1,0:T(8,128)(2,1)S(1)}, u32[]{:S(2)}, u32[]{:S(2)}) %collective-permute-start.25) | collective-permute-done | bytes 393248 | tf_op jit(solution)/shard_map/ppermute | solution.py:45
  159.8 3.7 %collective-permute-done.26 = bf16[2,96,1024]{2,1,0:T(8,128)(2,1)S(1)} collective-permute-done((bf16[2,96,1024]{2,1,0:T(8,128)(2,1)S(1)}, bf16[2,96,1024]{2,1,0:T(8,128)(2,1)S(1)}, u32[]{:S(2)}, u32[]{:S(2)}) %collective-permute-start.26) | collective-permute-done | bytes 393248 | tf_op jit(solution)/shard_map/ppermute | solution.py:45
  163.4 1.6 fusion.12
  (133 shorter events, 22.7 us)
Async XLA Ops:
  0.6 7.9 %copy-start.1 = (bf16[1,192,2560]{2,1,0:T(8,128)(2,1)S(1)}, bf16[1,192,2560]{2,1,0:T(8,128)(2,1)}, u32[]{:S(2)}) copy-start(bf16[1,192,2560]{2,1,0:T(8,128)(2,1)} %param.10) | copy-start | bytes 2949124
  5.5 12.5 %collective-permute-start = (bf16[192,1024]{1,0:T(8,128)(2,1)}, bf16[192,1024]{1,0:T(8,128)(2,1)S(1)}, u32[]{:S(2)}, u32[]{:S(2)}) collective-permute-start(bf16[192,1024]{1,0:T(8,128)(2,1)} %get-tuple-element.67), channel_id=1, source_target_pairs={{0,3},{1,2},{2,1},{3,0},{4,5},{5,4},{6,7},{7,6},{8,11},{9,10},{10,... | collective-permute-start | bytes 1179656 | tf_op jit(solution)/shard_map/ppermute | solution.py:45
  8.6 1.1 copy-start.9
  9.6 34.9 %collective-permute-start.17 = (bf16[2,192,640]{2,1,0:T(8,128)(2,1)}, bf16[2,192,640]{2,1,0:T(8,128)(2,1)}, u32[]{:S(2)}, u32[]{:S(2)}) collective-permute-start(bf16[2,192,640]{2,1,0:T(8,128)(2,1)} %pad_maximum_fusion.11), channel_id=1, source_target_pairs={{0,1},{1,0},{2,3},{3,2},{4,7},{5,6},{6,5},{7,4},{8,9},{9,8},{10,11... | collective-permute-start | bytes 1474568 | tf_op jit(solution)/shard_map/ppermute | solution.py:45
  9.8 11.9 %copy-start = (bf16[1,4,1024,640]{3,2,1,0:T(8,128)(2,1)S(1)}, bf16[1,4,1024,640]{3,2,1,0:T(8,128)(2,1)}, u32[]{:S(2)}) copy-start(bf16[1,4,1024,640]{3,2,1,0:T(8,128)(2,1)} %param.13) | copy-start | bytes 15728644
  19.1 12.1 %collective-permute-start.1 = (bf16[2,192,1024]{2,1,0:T(8,128)(2,1)S(1)}, bf16[2,192,1024]{2,1,0:T(8,128)(2,1)S(1)}, u32[]{:S(2)}, u32[]{:S(2)}) collective-permute-start(bf16[2,192,1024]{2,1,0:T(8,128)(2,1)S(1)} %pad_maximum_fusion.6), channel_id=1, source_target_pairs={{0,1},{1,0},{2,3},{3,2},{4,7},{5,6},{6,5},{7,4},{8,9},{9,8},{10,11... | collective-permute-start | bytes 2359304 | tf_op jit(solution)/shard_map/ppermute | solution.py:45
  31.2 3.4 %copy-start.2 = (bf16[192,1024]{1,0:T(8,128)(2,1)}, bf16[192,1024]{1,0:T(8,128)(2,1)S(1)}, u32[]{:S(2)}) copy-start(bf16[192,1024]{1,0:T(8,128)(2,1)S(1)} %slice_bitcast_fusion) | copy-start | bytes 1179652
  31.3 3.3 %copy-start.4 = (bf16[192,1024]{1,0:T(8,128)(2,1)}, bf16[192,1024]{1,0:T(8,128)(2,1)S(1)}, u32[]{:S(2)}) copy-start(bf16[192,1024]{1,0:T(8,128)(2,1)S(1)} %get-tuple-element.4) | copy-start | bytes 1179652
  31.3 3.3 %copy-start.6 = (bf16[192,1024]{1,0:T(8,128)(2,1)}, bf16[192,1024]{1,0:T(8,128)(2,1)S(1)}, u32[]{:S(2)}) copy-start(bf16[192,1024]{1,0:T(8,128)(2,1)S(1)} %get-tuple-element.5) | copy-start | bytes 1179652
  36.3 2.6 %collective-permute-start.9 = (bf16[2,4,96,640]{3,2,1,0:T(8,128)(2,1)S(1)}, bf16[2,4,96,640]{3,2,1,0:T(8,128)(2,1)S(1)}, u32[]{:S(2)}, u32[]{:S(2)}) collective-permute-start(bf16[2,4,96,640]{3,2,1,0:T(8,128)(2,1)S(1)} %fusion.58), channel_id=1, source_target_pairs={{0,4},{4,0},{8,12},{12,8},{16,20},{20,16},{24,28},{28,24},{1,5},{5... | collective-permute-start | bytes 2949128 | tf_op jit(solution)/shard_map/ppermute | solution.py:28
  36.8 0.7 copy-start.10
  36.8 0.9 copy-start.8
  37.0 3.4 %collective-permute-start.2 = (bf16[2,4,96,640]{3,2,1,0:T(8,128)(2,1)S(1)}, bf16[2,4,96,640]{3,2,1,0:T(8,128)(2,1)S(1)}, u32[]{:S(2)}, u32[]{:S(2)}) collective-permute-start(bf16[2,4,96,640]{3,2,1,0:T(8,128)(2,1)S(1)} %fusion.62), channel_id=1, source_target_pairs={{0,4},{4,0},{8,12},{12,8},{16,20},{20,16},{24,28},{28,24},{1,5},{5... | collective-permute-start | bytes 2949128 | tf_op jit(solution)/shard_map/ppermute | solution.py:28
  42.2 9.1 %collective-permute-start.3 = (bf16[2,2,4,24,640]{4,3,2,1,0:T(8,128)(2,1)}, bf16[2,2,4,24,640]{4,3,2,1,0:T(8,128)(2,1)}, u32[]{:S(2)}, u32[]{:S(2)}) collective-permute-start(bf16[2,2,4,24,640]{4,3,2,1,0:T(8,128)(2,1)} %pad_maximum_fusion.7), channel_id=1, source_target_pairs={{0,8},{4,28},{8,0},{12,20},{16,24},{20,12},{24,16},{28,4},{1,9},{5... | collective-permute-start | bytes 1474568 | tf_op jit(solution)/shard_map/ppermute | solution.py:45
  42.7 15.1 %collective-permute-start.10 = (bf16[2,2,4,24,640]{4,3,2,1,0:T(8,128)(2,1)S(1)}, bf16[2,2,4,24,640]{4,3,2,1,0:T(8,128)(2,1)S(1)}, u32[]{:S(2)}, u32[]{:S(2)}) collective-permute-start(bf16[2,2,4,24,640]{4,3,2,1,0:T(8,128)(2,1)S(1)} %pad_maximum_fusion.9), channel_id=1, source_target_pairs={{0,8},{4,28},{8,0},{12,20},{16,24},{20,12},{24,16},{28,4},{1,9},{5... | collective-permute-start | bytes 1474568 | tf_op jit(solution)/shard_map/ppermute | solution.py:45
  52.4 7.5 %collective-permute-start.4 = (bf16[2,4,24,640]{3,2,1,0:T(8,128)(2,1)S(1)}, bf16[2,4,24,640]{3,2,1,0:T(8,128)(2,1)S(1)}, u32[]{:S(2)}, u32[]{:S(2)}) collective-permute-start(bf16[2,4,24,640]{3,2,1,0:T(8,128)(2,1)S(1)} %fusion.106), channel_id=1, source_target_pairs={{0,24},{4,12},{8,16},{12,4},{16,8},{20,28},{24,0},{28,20},{1,25},{... | collective-permute-start | bytes 737288 | tf_op jit(solution)/shard_map/ppermute | solution.py:45
  52.5 50.6 %collective-permute-start.18 = (bf16[2,192,640]{2,1,0:T(8,128)(2,1)S(1)}, bf16[2,192,640]{2,1,0:T(8,128)(2,1)S(1)}, u32[]{:S(2)}, u32[]{:S(2)}) collective-permute-start(bf16[2,192,640]{2,1,0:T(8,128)(2,1)S(1)} %pad_maximum_fusion.12), channel_id=1, source_target_pairs={{0,3},{1,2},{2,1},{3,0},{4,5},{5,4},{6,7},{7,6},{8,11},{9,10},{10,... | collective-permute-start | bytes 1474568 | tf_op jit(solution)/shard_map/ppermute | solution.py:45
  57.9 7.7 %collective-permute-start.11 = (bf16[2,4,24,640]{3,2,1,0:T(8,128)(2,1)S(1)}, bf16[2,4,24,640]{3,2,1,0:T(8,128)(2,1)S(1)}, u32[]{:S(2)}, u32[]{:S(2)}) collective-permute-start(bf16[2,4,24,640]{3,2,1,0:T(8,128)(2,1)S(1)} %fusion.103), channel_id=1, source_target_pairs={{0,24},{4,12},{8,16},{12,4},{16,8},{20,28},{24,0},{28,20},{1,25},{... | collective-permute-start | bytes 737288 | tf_op jit(solution)/shard_map/ppermute | solution.py:45
  60.9 31.4 %slice-start = ((s8[5242880]{0:T(1024)(128)(4,1)}), s8[4194304]{0:T(1024)(128)(4,1)S(1)}, s32[]{:S(2)}) async-start(s8[5242880]{0:T(1024)(128)(4,1)} %bitcast.345), calls=%async_computation | async-start | bytes 8388608
  61.0 6.3 %collective-permute-start.5 = (bf16[1,4,24,640]{3,2,1,0:T(8,128)(2,1)S(1)}, bf16[1,4,24,640]{3,2,1,0:T(8,128)(2,1)S(1)}, u32[]{:S(2)}, u32[]{:S(2)}) collective-permute-start(bf16[1,4,24,640]{3,2,1,0:T(8,128)(2,1)S(1)} %get-tuple-element.59), channel_id=1, source_target_pairs={{0,32},{32,0},{64,96},{96,64},{4,36},{36,4},{68,100},{100,68},{8,4... | collective-permute-start | bytes 368648 | tf_op jit(solution)/shard_map/ppermute | solution.py:45
  65.7 6.8 %collective-permute-start.12 = (bf16[2,4,24,640]{3,2,1,0:T(8,128)(2,1)S(1)}, bf16[2,4,24,640]{3,2,1,0:T(8,128)(2,1)S(1)}, u32[]{:S(2)}, u32[]{:S(2)}) collective-permute-start(bf16[2,4,24,640]{3,2,1,0:T(8,128)(2,1)S(1)} %fusion.105), channel_id=1, source_target_pairs={{0,32},{32,0},{64,96},{96,64},{4,100},{36,68},{68,36},{100,4},{8,4... | collective-permute-start | bytes 737288 | tf_op jit(solution)/shard_map/ppermute | solution.py:45
  67.4 15.7 %collective-permute-start.6 = (bf16[2,4,24,640]{3,2,1,0:T(8,128)(2,1)S(1)}, bf16[2,4,24,640]{3,2,1,0:T(8,128)(2,1)S(1)}, u32[]{:S(2)}, u32[]{:S(2)}) collective-permute-start(bf16[2,4,24,640]{3,2,1,0:T(8,128)(2,1)S(1)} %fusion.93), channel_id=1, source_target_pairs={{0,24},{4,12},{8,16},{12,4},{16,8},{20,28},{24,0},{28,20},{1,25},{... | collective-permute-start | bytes 737288 | tf_op jit(solution)/shard_map/ppermute | solution.py:45
  72.6 7.5 %collective-permute-start.13 = (bf16[2,4,24,640]{3,2,1,0:T(8,128)(2,1)S(1)}, bf16[2,4,24,640]{3,2,1,0:T(8,128)(2,1)S(1)}, u32[]{:S(2)}, u32[]{:S(2)}) collective-permute-start(bf16[2,4,24,640]{3,2,1,0:T(8,128)(2,1)S(1)} %add_convert_fusion.3), channel_id=1, source_target_pairs={{0,96},{32,64},{64,32},{96,0},{4,36},{36,4},{68,100},{100,68},{8,1... | collective-permute-start | bytes 737288 | tf_op jit(solution)/shard_map/ppermute | solution.py:45
  75.5 16.8 %slice-start.1 = ((s8[5242880]{0:T(1024)(128)(4,1)}), s8[1048576]{0:T(1024)(128)(4,1)S(1)}, s32[]{:S(2)}) async-start(s8[5242880]{0:T(1024)(128)(4,1)} %bitcast.345), calls=%async_computation.1 | async-start | bytes 2097152
  80.3 10.1 %collective-permute-start.14 = (bf16[2,4,24,640]{3,2,1,0:T(8,128)(2,1)S(1)}, bf16[2,4,24,640]{3,2,1,0:T(8,128)(2,1)S(1)}, u32[]{:S(2)}, u32[]{:S(2)}) collective-permute-start(bf16[2,4,24,640]{3,2,1,0:T(8,128)(2,1)S(1)} %get-tuple-element.3), channel_id=1, source_target_pairs={{0,24},{4,12},{8,16},{12,4},{16,8},{20,28},{24,0},{28,20},{1,25},{... | collective-permute-start | bytes 737288 | tf_op jit(solution)/shard_map/ppermute | solution.py:45
  83.1 8.9 %collective-permute-start.7 = (bf16[2,2,4,24,640]{4,3,2,1,0:T(8,128)(2,1)S(1)}, bf16[2,2,4,24,640]{4,3,2,1,0:T(8,128)(2,1)S(1)}, u32[]{:S(2)}, u32[]{:S(2)}) collective-permute-start(bf16[2,2,4,24,640]{4,3,2,1,0:T(8,128)(2,1)S(1)} %pad_maximum_fusion.8), channel_id=1, source_target_pairs={{0,8},{4,28},{8,0},{12,20},{16,24},{20,12},{24,16},{28,4},{1,9},{5... | collective-permute-start | bytes 1474568 | tf_op jit(solution)/shard_map/ppermute | solution.py:45
  90.5 8.9 %collective-permute-start.15 = (bf16[2,2,4,24,640]{4,3,2,1,0:T(8,128)(2,1)S(1)}, bf16[2,2,4,24,640]{4,3,2,1,0:T(8,128)(2,1)S(1)}, u32[]{:S(2)}, u32[]{:S(2)}) collective-permute-start(bf16[2,2,4,24,640]{4,3,2,1,0:T(8,128)(2,1)S(1)} %pad_maximum_fusion.10), channel_id=1, source_target_pairs={{0,8},{4,28},{8,0},{12,20},{16,24},{20,12},{24,16},{28,4},{1,9},{5... | collective-permute-start | bytes 1474568 | tf_op jit(solution)/shard_map/ppermute | solution.py:45
  92.2 22.7 %collective-permute-start.8 = (bf16[2,384,640]{2,1,0:T(8,128)(2,1)S(1)}, bf16[2,384,640]{2,1,0:T(8,128)(2,1)S(1)}, u32[]{:S(2)}, u32[]{:S(2)}) collective-permute-start(bf16[2,384,640]{2,1,0:T(8,128)(2,1)S(1)} %bitcast.358), channel_id=1, source_target_pairs={{0,4},{4,0},{8,12},{12,8},{16,20},{20,16},{24,28},{28,24},{1,5},{5... | collective-permute-start | bytes 2949128 | tf_op jit(solution)/shard_map/ppermute | solution.py:28
  101.2 10.0 %collective-permute-start.19 = (bf16[2,96,1024]{2,1,0:T(8,128)(2,1)S(1)}, bf16[2,96,1024]{2,1,0:T(8,128)(2,1)S(1)}, u32[]{:S(2)}, u32[]{:S(2)}) collective-permute-start(bf16[2,96,1024]{2,1,0:T(8,128)(2,1)S(1)} %constant_dynamic-slice_fusion.1), channel_id=1, source_target_pairs={{0,1},{1,0},{2,3},{3,2},{4,7},{5,6},{6,5},{7,4},{8,9},{9,8},{10,11... | collective-permute-start | bytes 1179656 | tf_op jit(solution)/shard_map/ppermute | solution.py:45
  103.2 19.5 %collective-permute-start.16 = (bf16[2,384,640]{2,1,0:T(8,128)(2,1)S(1)}, bf16[2,384,640]{2,1,0:T(8,128)(2,1)S(1)}, u32[]{:S(2)}, u32[]{:S(2)}) collective-permute-start(bf16[2,384,640]{2,1,0:T(8,128)(2,1)S(1)} %bitcast.357), channel_id=1, source_target_pairs={{0,4},{4,0},{8,12},{12,8},{16,20},{20,16},{24,28},{28,24},{1,5},{5... | collective-permute-start | bytes 2949128 | tf_op jit(solution)/shard_map/ppermute | solution.py:28
  111.2 25.7 %collective-permute-start.20 = (bf16[96,1024]{1,0:T(8,128)(2,1)S(1)}, bf16[96,1024]{1,0:T(8,128)(2,1)S(1)}, u32[]{:S(2)}, u32[]{:S(2)}) collective-permute-start(bf16[96,1024]{1,0:T(8,128)(2,1)S(1)} %fusion.150), channel_id=1, source_target_pairs={{0,3},{1,2},{2,1},{3,0},{4,5},{5,4},{6,7},{7,6},{8,11},{9,10},{10,... | collective-permute-start | bytes 589832 | tf_op jit(solution)/shard_map/ppermute | solution.py:45
  116.5 1.0 copy-start.3
  116.5 1.1 copy-start.5
  116.5 1.2 copy-start.7
  124.3 9.4 %collective-permute-start.22 = (bf16[2,96,1024]{2,1,0:T(8,128)(2,1)S(1)}, bf16[2,96,1024]{2,1,0:T(8,128)(2,1)S(1)}, u32[]{:S(2)}, u32[]{:S(2)}) collective-permute-start(bf16[2,96,1024]{2,1,0:T(8,128)(2,1)S(1)} %constant_dynamic-slice_fusion), channel_id=1, source_target_pairs={{0,1},{1,0},{2,3},{3,2},{4,7},{5,6},{6,5},{7,4},{8,9},{9,8},{10,11... | collective-permute-start | bytes 1179656 | tf_op jit(solution)/shard_map/ppermute | solution.py:45
  133.8 8.8 %collective-permute-start.23 = (bf16[96,1024]{1,0:T(8,128)(2,1)S(1)}, bf16[96,1024]{1,0:T(8,128)(2,1)S(1)}, u32[]{:S(2)}, u32[]{:S(2)}) collective-permute-start(bf16[96,1024]{1,0:T(8,128)(2,1)S(1)} %fusion.151), channel_id=1, source_target_pairs={{0,3},{1,2},{2,1},{3,0},{4,5},{5,4},{6,7},{7,6},{8,11},{9,10},{10,... | collective-permute-start | bytes 589832 | tf_op jit(solution)/shard_map/ppermute | solution.py:45
  143.1 8.2 %collective-permute-start.21 = (bf16[96,1024]{1,0:T(8,128)(2,1)S(1)}, bf16[96,1024]{1,0:T(8,128)(2,1)S(1)}, u32[]{:S(2)}, u32[]{:S(2)}) collective-permute-start(bf16[96,1024]{1,0:T(8,128)(2,1)S(1)} %get-tuple-element.32), channel_id=1, source_target_pairs={{0,3},{1,2},{2,1},{3,0},{4,5},{5,4},{6,7},{7,6},{8,11},{9,10},{10,... | collective-permute-start | bytes 589832 | tf_op jit(solution)/shard_map/ppermute | solution.py:45
  145.7 8.7 %collective-permute-start.24 = (bf16[96,1024]{1,0:T(8,128)(2,1)S(1)}, bf16[96,1024]{1,0:T(8,128)(2,1)S(1)}, u32[]{:S(2)}, u32[]{:S(2)}) collective-permute-start(bf16[96,1024]{1,0:T(8,128)(2,1)S(1)} %get-tuple-element.33), channel_id=1, source_target_pairs={{0,3},{1,2},{2,1},{3,0},{4,5},{5,4},{6,7},{7,6},{8,11},{9,10},{10,... | collective-permute-start | bytes 589832 | tf_op jit(solution)/shard_map/ppermute | solution.py:45
  151.4 7.9 %collective-permute-start.25 = (bf16[2,96,1024]{2,1,0:T(8,128)(2,1)S(1)}, bf16[2,96,1024]{2,1,0:T(8,128)(2,1)S(1)}, u32[]{:S(2)}, u32[]{:S(2)}) collective-permute-start(bf16[2,96,1024]{2,1,0:T(8,128)(2,1)S(1)} %pad_maximum_fusion.13), channel_id=1, source_target_pairs={{0,1},{1,0},{2,3},{3,2},{4,7},{5,6},{6,5},{7,4},{8,9},{9,8},{10,11... | collective-permute-start | bytes 1179656 | tf_op jit(solution)/shard_map/ppermute | solution.py:45
  154.5 9.0 %collective-permute-start.26 = (bf16[2,96,1024]{2,1,0:T(8,128)(2,1)S(1)}, bf16[2,96,1024]{2,1,0:T(8,128)(2,1)S(1)}, u32[]{:S(2)}, u32[]{:S(2)}) collective-permute-start(bf16[2,96,1024]{2,1,0:T(8,128)(2,1)S(1)} %pad_maximum_fusion.14), channel_id=1, source_target_pairs={{0,1},{1,0},{2,3},{3,2},{4,7},{5,6},{6,5},{7,4},{8,9},{9,8},{10,11... | collective-permute-start | bytes 1179656 | tf_op jit(solution)/shard_map/ppermute | solution.py:45
